TPU v7x, 128 devices: a whole 4x4x4 slice. The times are simulated.
128 devices in a mesh: row: 8 (over x, core), col: 16 (over y, z).
Axes of the slice: x: 4, y: 4, z: 4, core: 2. Of those that a mesh axis runs over, the one named last changes fastest.
Arguments:
- children: bfloat16 [20480, 10240], P('row', 'col'), may hold values from -6 to 6
- row_maps: int32 [2, 80], replicated, may hold values from 0 to 159, as said below
- col_maps: int32 [2, 80], replicated, may hold values from 0 to 159, as said below
- pairs: int32 [8192, 2], replicated, may hold values from 0 to 159, as said below
- lower_panel: bfloat16 [20480, 1024], P('row', 'col'), may hold values from -6 to 6
- upper_panel: bfloat16 [1024, 20480], P('row', 'col'), may hold values from -0.1875 to 0.1875
Outputs:
- front: float32 [20480, 20480], P('row', 'col')
Inputs may be any that keep to these rules, and one draw needn't show every extreme that they name: Parent tile row r of the front's order is stored at tile row (r % 8) * 20 + r // 8. In the front's order each row of row_maps is increasing, child tile row i going to parent tile row 2 * i or 2 * i + 1. Of the 20 child tile rows b * 20 to b * 20 + 19 of one child, at most 5 map into any one stored block of tile rows a * 20 to a * 20 + 19, and in every such group of rows some block receives 5. Parent tile column r of the front's order is stored at tile column (r % 16) * 10 + r // 16. In the front's order each row of col_maps is increasing, child tile column j going to parent tile column 2 * j or 2 * j + 1. Of the 5 child tile columns b * 5 to b * 5 + 4 of one child, at most 1 map into any one stored block of tile columns a * 10 to a * 10 + 9, and in every such group some block receives 1. `pairs`: no pair is listed twice.
All inputs are finite; a program needn't handle non-finite values.
Results may differ from a plain program's by a relative error of at most 0.0003.
Values may be sent and summed in bfloat16 or wider, within the bound.
No kernel may reach another device: no remote copies, remote signals or barrier semaphores. Data moves between devices by JAX's collectives and lax.ppermute only.
A program may use at most 192 MiB of HBM per device.

v0:
```python
import jax
import jax.numpy as jnp
import numpy as np
from jax import lax
from jax.experimental import pallas as pl
from jax.experimental.pallas import tpu as pltpu
from jax.sharding import PartitionSpec as P


TILE = 128
COLS = 16
ROWS = 8
XS = 4
CT = 80
KC = 5
KR = 5
PRB = 20
PC = 10
ROUNDS = 5


def column_plan():
    holder, crossing, taken = {}, [], set()
    for m in range(8):
        side = []
        for k in range(PC):
            z = (m + 8 * k) // KC % 4
            if z // 2 == m % 2:
                side.append(z % 2)
            else:
                side.append({1: 0, 2: 1, 0: 1, 3: 0}[z])
        while sum(side) != ROUNDS:
            heavy = 0 if sum(side) < ROUNDS else 1
            for k in range(PC):
                z = (m + 8 * k) // KC % 4
                source = (m + 8 * k) // KC
                if side[k] == heavy and z // 2 == m % 2 and source not in taken:
                    side[k] = 1 - heavy
                    taken.add(source)
                    crossing.append(m + 8 * k)
                    break
        for k in range(PC):
            holder[m + 8 * k] = 2 * m + side[k]
    left = set(range(CT))
    rounds = []
    for r in range(ROUNDS):
        owner = {holder[j]: j for j in crossing} if r == 0 else {}
        fixed = {j // KC for j in owner.values()}

        def place(source, seen):
            for j in range(source * KC, source * KC + KC):
                target = holder[j]
                if j not in left or target in seen:
                    continue
                seen.add(target)
                free = target not in owner
                if not free and owner[target] // KC in fixed:
                    continue
                if free or place(owner[target] // KC, seen):
                    owner[target] = j
                    return True
            return False

        for source in range(COLS):
            assert source in fixed or place(source, set())
        rounds.append(dict(owner))
        left -= set(owner.values())
    assert not left
    return rounds


def pack_kernel(where, children, *outs):
    for r in range(ROUNDS):
        start = pl.multiple_of(where[XS + r] * TILE, TILE)
        for g in range(XS):
            for kk in range(KR):
                outs[r * XS + g][kk] = children[kk, where[g], :, pl.ds(start, TILE)]


def pack(children, where):
    spec = pltpu.PrefetchScalarGridSpec(
        num_scalar_prefetch=1,
        grid=(1,),
        in_specs=[pl.BlockSpec((KR, XS, TILE, KC * TILE), lambda i, w: (0, 0, 0, 0))],
        out_specs=[pl.BlockSpec((KR, TILE, TILE), lambda i, w: (0, 0, 0))] * (ROUNDS * XS),
    )
    return pl.pallas_call(
        pack_kernel,
        grid_spec=spec,
        out_shape=[jax.ShapeDtypeStruct((KR, TILE, TILE), jnp.bfloat16)] * (ROUNDS * XS),
        compiler_params=pltpu.CompilerParams(vmem_limit_bytes=32 << 20),
        cost_estimate=pl.CostEstimate(flops=0, bytes_accessed=6553600, transcendentals=0),
        name="pack",
    )(where, children.reshape(KR, XS, TILE, KC * TILE))


CORE, X_LO, X_HI, SLOT, COL_ON, ROW_ON = 0, 1, 2, 4, 14, 34
UNIT = (2, 1, KR, TILE, TILE)
HEIGHT = KR * TILE


def half_of(matches, block, scal):
    return jnp.where(matches, block // 2, jnp.maximum(block - 1, 0) // 2) ^ scal[X_LO]


def own_map(b, s):
    return (0, half_of(s[CORE] == b % 2, b, s), 0, 0, 0)


def other_map(b, s):
    return (0, half_of(s[CORE] != b % 2, b, s), 0, 0, 0)


def add_unit(scal, spot, block, unit, out, start):
    for g in range(2):
        child = g ^ scal[X_HI]

        @pl.when(scal[COL_ON + spot * 2 + g] == 1)
        def _():
            for kk in range(KR):

                @pl.when(scal[ROW_ON + child * PRB + block * KR + kk] == 1)
                def _():
                    rows = pl.ds(kk * TILE, TILE)
                    out[rows, pl.ds(start, TILE)] += unit[g, 0, kk].astype(jnp.float32)


def base_kernel(spots, scal, listed, lower, upper, *refs):
    units, out = refs[:-1], refs[-1]
    block = pl.program_id(0)
    same = block % 2 == scal[CORE]
    for kk in range(KR):
        rows = pl.ds(kk * TILE, TILE)
        acc = jnp.dot(lower[rows, :], upper[...], preferred_element_type=jnp.float32)
        out[rows, :] = jnp.where(listed[block * KR + kk] > 0.5, -acc, 0.0)

    def add(group):
        for spot, unit in zip(spots, group):
            start = pl.multiple_of(scal[SLOT + spot] * TILE, TILE)
            add_unit(scal, spot, block, unit, out, start)

    @pl.when(same)
    def _():
        add(units[: len(spots)])

    @pl.when(jnp.logical_not(same))
    def _():
        add(units[len(spots) :])


def base(scal, listed, lower, upper, spots, own, other):
    n = len(spots)
    spec = pltpu.PrefetchScalarGridSpec(
        num_scalar_prefetch=1,
        grid=(PRB // KR,),
        in_specs=[
            pl.BlockSpec((PRB, 1, PC * TILE), lambda b, s: (0, 0, 0)),
            pl.BlockSpec((HEIGHT, 1024), lambda b, s: (b, 0)),
            pl.BlockSpec((1024, PC * TILE), lambda b, s: (0, 0)),
        ]
        + [pl.BlockSpec(UNIT, own_map)] * n
        + [pl.BlockSpec(UNIT, other_map)] * n,
        out_specs=pl.BlockSpec((HEIGHT, PC * TILE), lambda b, s: (b, 0)),
    )

    def kernel(*refs):
        base_kernel(spots, *refs)

    return pl.pallas_call(
        kernel,
        grid_spec=spec,
        out_shape=jax.ShapeDtypeStruct((PRB * TILE, PC * TILE), jnp.float32),
        compiler_params=pltpu.CompilerParams(vmem_limit_bytes=56 << 20),
        cost_estimate=pl.CostEstimate(
            flops=2 * 2560 * 1280 * 1024, bytes_accessed=34 << 20, transcendentals=0
        ),
        name="base",
    )(scal, listed, lower, upper, *own, *other)


def tail(scal, front, spots, own, other):
    n = len(spots)

    def kernel(scal, *refs):
        units, fronts, out = refs[: 2 * n], refs[2 * n], refs[2 * n + 1]
        block = pl.program_id(1)
        same = block % 2 == scal[CORE]
        out[...] = fronts[...]
        for i, spot in enumerate(spots):

            @pl.when((pl.program_id(0) == i) & same)
            def _():
                add_unit(scal, spot, block, units[i], out, 0)

            @pl.when((pl.program_id(0) == i) & jnp.logical_not(same))
            def _():
                add_unit(scal, spot, block, units[n + i], out, 0)

    def front_map(i, b, s):
        slot = s[SLOT + spots[0]]
        for j in range(1, n):
            slot = jnp.where(i == j, s[SLOT + spots[j]], slot)
        return (b, slot)

    def unit_map(index, pick):
        def at(i, b, s):
            now = jnp.where(i == index, b, jnp.where(i < index, 0, PRB // KR - 1))
            return pick(now, s)

        return at

    spec = pltpu.PrefetchScalarGridSpec(
        num_scalar_prefetch=1,
        grid=(n, PRB // KR),
        in_specs=[pl.BlockSpec(UNIT, unit_map(i, own_map)) for i in range(n)]
        + [pl.BlockSpec(UNIT, unit_map(i, other_map)) for i in range(n)]
        + [pl.BlockSpec((HEIGHT, TILE), front_map)],
        out_specs=pl.BlockSpec((HEIGHT, TILE), front_map),
    )
    return pl.pallas_call(
        kernel,
        grid_spec=spec,
        out_shape=jax.ShapeDtypeStruct((PRB * TILE, PC * TILE), jnp.float32),
        input_output_aliases={2 * n + 1: 0},
        compiler_params=pltpu.CompilerParams(vmem_limit_bytes=32 << 20),
        cost_estimate=pl.CostEstimate(flops=0, bytes_accessed=8 << 20, transcendentals=0),
        name="tail",
    )(scal, *own, *other, front)


def hop(array, row_mask=0, col_mask=0):
    route = [
        (p * COLS + q, (p ^ row_mask) * COLS + (q ^ col_mask))
        for p in range(ROWS)
        for q in range(COLS)
    ]
    return lax.ppermute(array, ("row", "col"), route)


def compute(children, row_maps, col_maps, pairs, lower_panel, upper_panel):
    row = lax.axis_index("row")
    col = lax.axis_index("col")
    chip, core = row >> 1, row & 1
    rounds = column_plan()
    source_of = [[0] * COLS for _ in range(ROUNDS)]
    tile_of = np.zeros((ROUNDS, COLS), np.int32)
    slot_of = np.zeros((ROUNDS, COLS), np.int32)
    for r, owner in enumerate(rounds):
        for target, j in owner.items():
            source_of[r][target] = j // KC
            tile_of[r, j // KC] = j % KC
            slot_of[r, target] = j // 8

    low = lower_panel.T
    low_z1 = hop(low, col_mask=1)
    low01 = jnp.concatenate([low, low_z1])
    low32 = hop(low01, col_mask=3)
    low_here = jnp.concatenate([low01, low32])
    low_y1 = hop(low_here, col_mask=4)
    low_y3 = hop(low_here, col_mask=12)
    low_y2a = hop(low_y1[:128], col_mask=12)
    low_y2b = hop(low_y3[128:], col_mask=4)
    lower_all = jnp.concatenate([low_here, low_y1, low_y2a, low_y2b, low_y3]).T
    piece_col = col ^ (
        4 * jnp.asarray([0, 1, 2, 3], jnp.int32)[:, None]
        + jnp.asarray([0, 1, 3, 2], jnp.int32)[None, :]
    ).reshape(-1)

    up_x1 = hop(upper_panel, row_mask=2)
    up01 = jnp.concatenate([upper_panel, up_x1])
    up32 = hop(up01, row_mask=6)
    up_here = jnp.concatenate([up01, up32])
    up_core = hop(up_here, row_mask=1)
    up_pieces = jnp.concatenate([up_here, up_core]).reshape(2, XS, 2, 64, PC * TILE)
    piece_row = row ^ (piece_col >> 1)
    flip = piece_row >> 1
    place = jnp.where(flip == 2, 3, jnp.where(flip == 3, 2, flip))
    index = ((piece_row & 1) * XS + place) * 2 + (piece_col & 1)
    upper_all = jnp.take(up_pieces.reshape(16, 64, PC * TILE), index, axis=0, mode="clip")
    upper_all = upper_all.reshape(1024, PC * TILE)

    where = jnp.concatenate(
        [chip ^ jnp.arange(XS, dtype=jnp.int32), jnp.asarray(tile_of)[:, col]]
    ).astype(jnp.int32)
    packed = pack(children, where)

    held, swapped, core_held, core_swapped = [], [], [], []
    for r in range(ROUNDS):
        got = []
        for g in range(XS):
            route = [
                (p * COLS + source_of[r][q], (p ^ (2 * g)) * COLS + q)
                for p in range(ROWS)
                for q in range(COLS)
            ]
            got.append(lax.ppermute(packed[r * XS + g], ("row", "col"), route))
        held.append(jnp.stack(got).reshape(2, 2, KR, TILE, TILE))
    for r in range(ROUNDS):
        swapped.append(hop(held[r], col_mask=1))
        core_held.append(hop(held[r], row_mask=1))
        core_swapped.append(hop(swapped[r], row_mask=1))

    slots = jnp.arange(PRB, dtype=jnp.int32)
    row_on = lax.dynamic_slice_in_dim(row_maps.reshape(2, PRB, XS), chip, 1, 2)[:, :, 0]
    row_on = (row_on == row * PRB + slots).astype(jnp.int32)
    spots = jnp.arange(PC, dtype=jnp.int32)
    col_on = lax.dynamic_slice_in_dim(col_maps.reshape(2, PC, 8), col >> 1, 1, 2)[:, :, 0]
    col_on = (col_on == col * PC + spots).astype(jnp.int32)
    slot = jnp.concatenate([jnp.asarray(slot_of)[:, col], jnp.asarray(slot_of)[:, col ^ 1]])
    sides = (chip >> 1) ^ jnp.arange(2, dtype=jnp.int32)
    by_slot = jnp.sum(
        jnp.where(slot[:, None] == spots[None, :], 1, 0)[:, None, :] * col_on[sides][None], axis=2
    )
    scal = jnp.concatenate(
        [
            jnp.stack([core, chip & 1, chip >> 1, chip]),
            slot,
            by_slot.reshape(-1),
            row_on.reshape(-1),
        ]
    ).astype(jnp.int32)

    row_hit = (pairs[:, 0][:, None] == row * PRB + slots[None, :]).astype(jnp.bfloat16)
    col_hit = (pairs[:, 1][:, None] == col * PC + spots[None, :]).astype(jnp.bfloat16)
    listed = jnp.dot(row_hit.T, col_hit, preferred_element_type=jnp.float32)
    listed = jnp.repeat(listed, TILE, axis=1).reshape(PRB, 1, PC * TILE)

    own = held + swapped
    other = core_held + core_swapped
    early = list(range(2 * ROUNDS - 2))
    late = [2 * ROUNDS - 2, 2 * ROUNDS - 1]
    front = base(
        scal,
        listed,
        lower_all,
        upper_all,
        early,
        [own[i] for i in early],
        [other[i] for i in early],
    )
    return tail(scal, front, late, [own[i] for i in late], [other[i] for i in late])


def solution(mesh):
    placed = (P("row", "col"), P(), P(), P(), P("row", "col"), P("row", "col"))
    return jax.shard_map(
        compute, mesh=mesh, in_specs=placed, out_specs=P("row", "col"), check_vma=False
    )
```

profile of v0, /device:TPU:49, one launch (start us, length us, event | category | flops | bytes accessed | tf_op | source)
XLA Modules:
  0.0 214.2 jit_solution(10949054146037102016)
XLA Ops:
  0.0 0.8 fusion.11
  0.9 1.9 copy-done
  2.8 1.1 pack.1
  3.9 1.7 collective-permute-start.21
  5.6 1.0 collective-permute-start.22
  6.6 1.9 collective-permute-start.23
  8.5 2.3 %collective-permute-start.24 = (bf16[5,128,128]{2,1,0:T(8,128)(2,1)S(1)}, bf16[5,128,128]{2,1,0:T(8,128)(2,1)}, u32[]{:S(2)}, u32[]{:S(2)}) collective-permute-start(bf16[5,128,128]{2,1,0:T(8,128)(2,1)S(1)} %get-tuple-element.36), channel_id=1, source_target_pairs={{8,96},{0,97},{13,98},{6,99},{5,100},{10,101},{3,102},{15,103},{12... | collective-permute-start | bytes 491528 | tf_op jit(solution)/shard_map/ppermute | solution.py:296
  10.8 2.6 %collective-permute-start.25 = (bf16[5,128,128]{2,1,0:T(8,128)(2,1)S(1)}, bf16[5,128,128]{2,1,0:T(8,128)(2,1)}, u32[]{:S(2)}, u32[]{:S(2)}) collective-permute-start(bf16[5,128,128]{2,1,0:T(8,128)(2,1)S(1)} %get-tuple-element.37), channel_id=1, source_target_pairs={{11,0},{9,1},{5,2},{8,3},{0,4},{13,5},{2,6},{7,7},{15,8},{10,9},{1... | collective-permute-start | bytes 491528 | tf_op jit(solution)/shard_map/ppermute | solution.py:296
  13.4 0.7 copy-done.18
  14.1 3.6 %collective-permute-start.12 = (bf16[64,2560]{1,0:T(8,128)(2,1)}, bf16[64,2560]{1,0:T(8,128)(2,1)}, u32[]{:S(2)}, u32[]{:S(2)}) collective-permute-start(bf16[64,2560]{1,0:T(8,128)(2,1)} %bitcast.22), channel_id=1, source_target_pairs={{0,1},{1,0},{2,3},{3,2},{4,5},{5,4},{6,7},{7,6},{8,9},{9,8},{10,11... | collective-permute-start | bytes 983048 | tf_op jit(solution)/shard_map/ppermute | solution.py:237
  17.7 2.1 copy.37
  19.8 3.5 %collective-permute-start.26 = (bf16[5,128,128]{2,1,0:T(8,128)(2,1)S(1)}, bf16[5,128,128]{2,1,0:T(8,128)(2,1)}, u32[]{:S(2)}, u32[]{:S(2)}) collective-permute-start(bf16[5,128,128]{2,1,0:T(8,128)(2,1)S(1)} %get-tuple-element.38), channel_id=1, source_target_pairs={{11,32},{9,33},{5,34},{8,35},{0,36},{13,37},{2,38},{7,39},{15,40},... | collective-permute-start | bytes 491528 | tf_op jit(solution)/shard_map/ppermute | solution.py:296
  23.3 10.3 %collective-permute-start.27 = (bf16[5,128,128]{2,1,0:T(8,128)(2,1)S(1)}, bf16[5,128,128]{2,1,0:T(8,128)(2,1)}, u32[]{:S(2)}, u32[]{:S(2)}) collective-permute-start(bf16[5,128,128]{2,1,0:T(8,128)(2,1)S(1)} %get-tuple-element.39), channel_id=1, source_target_pairs={{11,64},{9,65},{5,66},{8,67},{0,68},{13,69},{2,70},{7,71},{15,72},... | collective-permute-start | bytes 491528 | tf_op jit(solution)/shard_map/ppermute | solution.py:296
  33.7 1.9 collective-permute-start.29
  35.6 3.4 %collective-permute-start.30 = (bf16[5,128,128]{2,1,0:T(8,128)(2,1)S(1)}, bf16[5,128,128]{2,1,0:T(8,128)(2,1)}, u32[]{:S(2)}, u32[]{:S(2)}) collective-permute-start(bf16[5,128,128]{2,1,0:T(8,128)(2,1)S(1)} %get-tuple-element.42), channel_id=1, source_target_pairs={{3,32},{14,33},{9,34},{11,35},{8,36},{6,37},{5,38},{0,39},{7,40},{... | collective-permute-start | bytes 491528 | tf_op jit(solution)/shard_map/ppermute | solution.py:296
  39.1 1.3 copy.41
  40.4 2.8 %collective-permute-start.31 = (bf16[5,128,128]{2,1,0:T(8,128)(2,1)S(1)}, bf16[5,128,128]{2,1,0:T(8,128)(2,1)S(1)}, u32[]{:S(2)}, u32[]{:S(2)}) collective-permute-start(bf16[5,128,128]{2,1,0:T(8,128)(2,1)S(1)} %get-tuple-element.43), channel_id=1, source_target_pairs={{3,64},{14,65},{9,66},{11,67},{8,68},{6,69},{5,70},{0,71},{7,72},{... | collective-permute-start | bytes 491528 | tf_op jit(solution)/shard_map/ppermute | solution.py:296
  43.2 4.7 %collective-permute-start.32 = (bf16[5,128,128]{2,1,0:T(8,128)(2,1)S(1)}, bf16[5,128,128]{2,1,0:T(8,128)(2,1)S(1)}, u32[]{:S(2)}, u32[]{:S(2)}) collective-permute-start(bf16[5,128,128]{2,1,0:T(8,128)(2,1)S(1)} %get-tuple-element.44), channel_id=1, source_target_pairs={{3,96},{14,97},{9,98},{11,99},{8,100},{6,101},{5,102},{0,103},{7,1... | collective-permute-start | bytes 491528 | tf_op jit(solution)/shard_map/ppermute | solution.py:296
  47.9 1.9 collective-permute-start.5
  49.9 9.0 %collective-permute-done.29 = bf16[5,128,128]{2,1,0:T(8,128)(2,1)} collective-permute-done((bf16[5,128,128]{2,1,0:T(8,128)(2,1)S(1)}, bf16[5,128,128]{2,1,0:T(8,128)(2,1)}, u32[]{:S(2)}, u32[]{:S(2)}) %collective-permute-start.29) | collective-permute-done | bytes 163872 | tf_op jit(solution)/shard_map/ppermute | solution.py:296
  58.9 2.3 %pad_maximum_fusion.5 = bf16[128,2560]{0,1:T(8,128)(2,1)} fusion(bf16[64,2560]{0,1:T(8,128)(2,1)S(1)} %copy.41, bf16[64,2560]{0,1:T(8,128)(2,1)} %bitcast.50), kind=kLoop, calls=%fused_computation.9 | loop fusion | flops 1310720 | bytes 1310720 | tf_op jit(solution)/shard_map/concatenate | solution.py:256
  61.2 4.2 %collective-permute-start.13 = (bf16[128,2560]{0,1:T(8,128)(2,1)}, bf16[128,2560]{0,1:T(8,128)(2,1)}, u32[]{:S(2)}, u32[]{:S(2)}) collective-permute-start(bf16[128,2560]{0,1:T(8,128)(2,1)} %pad_maximum_fusion.5), channel_id=1, source_target_pairs={{0,3},{1,2},{2,1},{3,0},{4,7},{5,6},{6,5},{7,4},{8,11},{9,10},{10,... | collective-permute-start | bytes 1966088 | tf_op jit(solution)/shard_map/ppermute | solution.py:237
  65.5 2.1 pad_maximum_fusion.7
  67.6 1.8 collective-permute-done.5
  69.4 4.5 %collective-permute-start.8 = (bf16[5,128,128]{2,1,0:T(8,128)(2,1)S(1)}, bf16[5,128,128]{2,1,0:T(8,128)(2,1)S(1)}, u32[]{:S(2)}, u32[]{:S(2)}) collective-permute-start(bf16[5,128,128]{2,1,0:T(8,128)(2,1)S(1)} %get-tuple-element.32), channel_id=1, source_target_pairs={{12,96},{6,97},{1,98},{0,99},{3,100},{14,101},{10,102},{11,103},{8... | collective-permute-start | bytes 491528 | tf_op jit(solution)/shard_map/ppermute | solution.py:296
  73.9 1.6 collective-permute-start.2
  75.5 2.1 pad_maximum_fusion.8
  77.6 1.9 pad_maximum_fusion.9
  79.5 6.1 %collective-permute-start.3 = (bf16[5,128,128]{2,1,0:T(8,128)(2,1)S(1)}, bf16[5,128,128]{2,1,0:T(8,128)(2,1)S(1)}, u32[]{:S(2)}, u32[]{:S(2)}) collective-permute-start(bf16[5,128,128]{2,1,0:T(8,128)(2,1)S(1)} %get-tuple-element.28), channel_id=1, source_target_pairs={{4,96},{1,97},{14,98},{3,99},{11,100},{2,101},{13,102},{8,103},{0,... | collective-permute-start | bytes 491528 | tf_op jit(solution)/shard_map/ppermute | solution.py:296
  85.6 4.0 %collective-permute-start = (bf16[5,128,128]{2,1,0:T(8,128)(2,1)S(1)}, bf16[5,128,128]{2,1,0:T(8,128)(2,1)}, u32[]{:S(2)}, u32[]{:S(2)}) collective-permute-start(bf16[5,128,128]{2,1,0:T(8,128)(2,1)S(1)} %get-tuple-element.25), channel_id=1, source_target_pairs={{4,0},{1,1},{14,2},{3,3},{11,4},{2,5},{13,6},{8,7},{0,8},{5,9},{10... | collective-permute-start | bytes 491528 | tf_op jit(solution)/shard_map/ppermute | solution.py:296
  89.7 1.4 collective-permute-start.34
  91.2 0.9 pad_maximum_fusion.6
  92.2 2.1 collective-permute-done
  94.8 6.6 %collective-permute-start.36 = (bf16[2,2,5,128,128]{4,3,2,1,0:T(8,128)(2,1)}, bf16[2,2,5,128,128]{4,3,2,1,0:T(8,128)(2,1)S(1)}, u32[]{:S(2)}, u32[]{:S(2)}) collective-permute-start(bf16[2,2,5,128,128]{4,3,2,1,0:T(8,128)(2,1)} %bitcast.31.refs_4_), channel_id=1, source_target_pairs={{0,16},{1,17},{2,18},{3,19},{4,20},{5,21},{6,22},{7,23},{8,24},{9,... | collective-permute-start | bytes 1966088 | tf_op jit(solution)/shard_map/ppermute | solution.py:237
  101.4 2.7 %pad_maximum_fusion.1 = bf16[256,2560]{0,1:T(8,128)(2,1)} fusion(bf16[128,2560]{0,1:T(8,128)(2,1)} %collective-permute-done.13, bf16[64,2560]{0,1:T(8,128)(2,1)S(1)} %copy.41, bf16[64,2560]{0,1:T(8,128)(2,1)S(1)} %bitcast.51), kind=kLoop, calls=%fused_computation.3 | loop fusion | flops 3932160 | bytes 2621440 | tf_op jit(solution)/shard_map/concatenate | solution.py:258
  104.2 1.0 collective-permute-start.14
  105.2 11.7 %collective-permute-done.34.refs_10_ = bf16[2,2,5,128,128]{4,3,2,1,0:T(8,128)(2,1)} collective-permute-done((bf16[2,2,5,128,128]{4,3,2,1,0:T(8,128)(2,1)}, bf16[2,2,5,128,128]{4,3,2,1,0:T(8,128)(2,1)}, u32[]{:S(2)}, u32[]{:S(2)}) %collective-permute-start.34) | collective-permute-done | bytes 655392 | tf_op jit(solution)/shard_map/ppermute | solution.py:237
  117.0 14.0 %collective-permute-done.35.refs_11_ = bf16[2,2,5,128,128]{4,3,2,1,0:T(8,128)(2,1)} collective-permute-done((bf16[2,2,5,128,128]{4,3,2,1,0:T(8,128)(2,1)}, bf16[2,2,5,128,128]{4,3,2,1,0:T(8,128)(2,1)}, u32[]{:S(2)}, u32[]{:S(2)}) %collective-permute-start.35) | collective-permute-done | bytes 655392 | tf_op jit(solution)/shard_map/ppermute | solution.py:237
  131.0 4.3 %collective-permute-start.37 = (bf16[2,2,5,128,128]{4,3,2,1,0:T(8,128)(2,1)}, bf16[2,2,5,128,128]{4,3,2,1,0:T(8,128)(2,1)S(1)}, u32[]{:S(2)}, u32[]{:S(2)}) collective-permute-start(bf16[2,2,5,128,128]{4,3,2,1,0:T(8,128)(2,1)} %bitcast.36.refs_5_), channel_id=1, source_target_pairs={{0,16},{1,17},{2,18},{3,19},{4,20},{5,21},{6,22},{7,23},{8,24},{9,... | collective-permute-start | bytes 1966088 | tf_op jit(solution)/shard_map/ppermute | solution.py:237
  135.3 0.3 collective-permute-start.38
  135.5 1.2 pad_maximum_fusion.2
  136.7 0.8 copy-done.9
  137.8 0.6 gather_fusion
  138.4 1.2 pad_maximum_fusion.4
  139.6 1.5 pad_maximum_fusion.3
  141.1 0.3 collective-permute-start.40
  142.0 1.4 collective-permute-start.4
  143.3 0.4 fusion
  143.7 2.0 slice.20
  145.7 2.0 slice.21
  147.7 0.8 copy-done.11
  148.5 0.8 copy-done.12
  150.5 0.7 reshape_reshape.8.refs_1_
  151.2 0.7 concatenate.33.refs_0_.scal
  151.9 6.1 %collective-permute-done.9.refs_1_ = bf16[2,2,5,128,128]{4,3,2,1,0:T(8,128)(2,1)S(1)} collective-permute-done((bf16[2,2,5,128,128]{4,3,2,1,0:T(8,128)(2,1)S(1)}, bf16[2,2,5,128,128]{4,3,2,1,0:T(8,128)(2,1)S(1)}, u32[]{:S(2)}, u32[]{:S(2)}) %collective-permute-start.9) | collective-permute-done | bytes 655392 | tf_op jit(solution)/shard_map/ppermute | solution.py:237
  158.0 1.7 collective-permute-start.41
  159.7 12.2 %collective-permute-done.4.refs_0_ = bf16[2,2,5,128,128]{4,3,2,1,0:T(8,128)(2,1)S(1)} collective-permute-done((bf16[2,2,5,128,128]{4,3,2,1,0:T(8,128)(2,1)S(1)}, bf16[2,2,5,128,128]{4,3,2,1,0:T(8,128)(2,1)S(1)}, u32[]{:S(2)}, u32[]{:S(2)}) %collective-permute-start.4) | collective-permute-done | bytes 655392 | tf_op jit(solution)/shard_map/ppermute | solution.py:237
  171.9 1.1 collective-permute-start.42
  173.1 0.6 collective-permute-start.11
  173.8 2.9 %pad_maximum_fusion = bf16[1024,1280]{1,0:T(8,128)(2,1)} fusion(bf16[512,1280]{1,0:T(8,128)(2,1)} %collective-permute-done.20, bf16[256,1280]{1,0:T(8,128)(2,1)} %copy-done.6, bf16[128,1280]{1,0:T(8,128)(2,1)} %copy-done.5, bf16[128,1280]{1,0:T(8,128)(2,1)} %param.15), kind=kLoop, calls=%fused_computation.2 | loop fusion | flops 10485760 | bytes 5242880 | tf_op jit(solution)/shard_map/concatenate | solution.py:274
  176.7 4.0 %gather_fusion.1 = bf16[16,64,1280]{2,1,0:T(8,128)(2,1)} fusion(bf16[16,64,1280]{2,1,0:T(8,128)(2,1)} %bitcast.49, s32[1024]{0:T(1024)S(1)} %pad_clamp_fusion), kind=kCustom, calls=%fused_computation.1 | custom fusion | bytes 5242944 | tf_op jit(solution)/shard_map/jit(_take)/gather | solution.py:279
  180.7 9.0 %concatenate.37 = bf16[1024,2560]{0,1:T(8,128)(2,1)} concatenate(bf16[64,2560]{0,1:T(8,128)(2,1)S(1)} %bitcast.52, bf16[64,2560]{0,1:T(8,128)(2,1)} %copy-done.3, bf16[128,2560]{0,1:T(8,128)(2,1)} %collective-permute-done.13, bf16[256,2560]{0,1:T(8,128)(2,1)} %collective-permute-done.14, bf16[128,2560]{0,1:T(8,128)(2,1)} %collective-permute-done.15, ...), dimensions={0} | concatenate | bytes 10485760 | tf_op jit(solution)/shard_map/concatenate | solution.py:263
  189.7 17.4 %base.1.refs_4_ = f32[2560,1280]{1,0:T(8,128)} custom-call(s32[74]{0:T(128)} %concatenate.33.refs_0_.scal, f32[20,1,1280]{2,1,0:T(1,128)} %reshape_reshape.8.refs_1_, bf16[2560,1024]{1,0:T(8,128)(2,1)} %bitcast.48, bf16[1024,1280]{1,0:T(8,128)(2,1)} %bitcast.53, bf16[2,2,5,128,128]{4,3,2,1,0:T(8,128)(2,1)} %bitcast.31.refs_4_, ...), custom_call_target="tpu_custom_call" | custom-call | flops 6710886400 | bytes 35651584 | tf_op jit(solution)/shard_map/base/pallas_call | solution.py:169
  207.2 7.0 %tail.1 = f32[2560,1280]{1,0:T(8,128)} custom-call(s32[74]{0:T(128)S(1)} %copy-done.1, bf16[2,2,5,128,128]{4,3,2,1,0:T(8,128)(2,1)S(1)} %collective-permute-done.4.refs_0_, bf16[2,2,5,128,128]{4,3,2,1,0:T(8,128)(2,1)S(1)} %collective-permute-done.9.refs_1_, ...), custom_call_target="tpu_custom_call", output_to_operand_aliasing={{}: (5, {})} | custom-call | bytes 8388608 | tf_op jit(solution)/shard_map/tail/pallas_call | solution.py:220
  (124 shorter events, 3.2 us)
Async XLA Ops:
  0.0 39.0 %copy-start.23 = (s32[4]{0:T(128)S(1)}, s32[4]{0:T(128)}, u32[]{:S(2)}) copy-start(s32[4]{0:T(128)} %constant.11.clone) | copy-start | bytes 52
  0.9 1.9 copy-start
  2.8 14.9 %copy-start.20 = (s32[8192,2]{0,1:T(2,128)S(1)}, s32[8192,2]{0,1:T(2,128)}, u32[]{:S(2)}) copy-start(s32[8192,2]{0,1:T(2,128)} %param.13) | copy-start | bytes 196612
  3.9 57.3 %copy-start.4 = (bf16[128,1280]{1,0:T(8,128)(2,1)S(1)}, bf16[128,1280]{1,0:T(8,128)(2,1)}, u32[]{:S(2)}) copy-start(bf16[128,1280]{1,0:T(8,128)(2,1)} %param.15) | copy-start | bytes 983044
  3.9 9.5 %collective-permute-start.21 = (bf16[5,128,128]{2,1,0:T(8,128)(2,1)S(1)}, bf16[5,128,128]{2,1,0:T(8,128)(2,1)S(1)}, u32[]{:S(2)}, u32[]{:S(2)}) collective-permute-start(bf16[5,128,128]{2,1,0:T(8,128)(2,1)S(1)} %get-tuple-element.33), channel_id=1, source_target_pairs={{8,0},{0,1},{13,2},{6,3},{5,4},{10,5},{3,6},{15,7},{12,8},{4,9},{9... | collective-permute-start | bytes 491528 | tf_op jit(solution)/shard_map/ppermute | solution.py:296
  5.6 14.2 %collective-permute-start.22 = (bf16[5,128,128]{2,1,0:T(8,128)(2,1)S(1)}, bf16[5,128,128]{2,1,0:T(8,128)(2,1)}, u32[]{:S(2)}, u32[]{:S(2)}) collective-permute-start(bf16[5,128,128]{2,1,0:T(8,128)(2,1)S(1)} %get-tuple-element.34), channel_id=1, source_target_pairs={{8,32},{0,33},{13,34},{6,35},{5,36},{10,37},{3,38},{15,39},{12,40}... | collective-permute-start | bytes 491528 | tf_op jit(solution)/shard_map/ppermute | solution.py:296
  6.6 16.7 %collective-permute-start.23 = (bf16[5,128,128]{2,1,0:T(8,128)(2,1)S(1)}, bf16[5,128,128]{2,1,0:T(8,128)(2,1)}, u32[]{:S(2)}, u32[]{:S(2)}) collective-permute-start(bf16[5,128,128]{2,1,0:T(8,128)(2,1)S(1)} %get-tuple-element.35), channel_id=1, source_target_pairs={{8,64},{0,65},{13,66},{6,67},{5,68},{10,69},{3,70},{15,71},{12,72}... | collective-permute-start | bytes 491528 | tf_op jit(solution)/shard_map/ppermute | solution.py:296
  8.5 25.2 %collective-permute-start.24 = (bf16[5,128,128]{2,1,0:T(8,128)(2,1)S(1)}, bf16[5,128,128]{2,1,0:T(8,128)(2,1)}, u32[]{:S(2)}, u32[]{:S(2)}) collective-permute-start(bf16[5,128,128]{2,1,0:T(8,128)(2,1)S(1)} %get-tuple-element.36), channel_id=1, source_target_pairs={{8,96},{0,97},{13,98},{6,99},{5,100},{10,101},{3,102},{15,103},{12... | collective-permute-start | bytes 491528 | tf_op jit(solution)/shard_map/ppermute | solution.py:296
  10.8 22.9 %collective-permute-start.25 = (bf16[5,128,128]{2,1,0:T(8,128)(2,1)S(1)}, bf16[5,128,128]{2,1,0:T(8,128)(2,1)}, u32[]{:S(2)}, u32[]{:S(2)}) collective-permute-start(bf16[5,128,128]{2,1,0:T(8,128)(2,1)S(1)} %get-tuple-element.37), channel_id=1, source_target_pairs={{11,0},{9,1},{5,2},{8,3},{0,4},{13,5},{2,6},{7,7},{15,8},{10,9},{1... | collective-permute-start | bytes 491528 | tf_op jit(solution)/shard_map/ppermute | solution.py:296
  14.1 21.6 %collective-permute-start.12 = (bf16[64,2560]{1,0:T(8,128)(2,1)}, bf16[64,2560]{1,0:T(8,128)(2,1)}, u32[]{:S(2)}, u32[]{:S(2)}) collective-permute-start(bf16[64,2560]{1,0:T(8,128)(2,1)} %bitcast.22), channel_id=1, source_target_pairs={{0,1},{1,0},{2,3},{3,2},{4,5},{5,4},{6,7},{7,6},{8,9},{9,8},{10,11... | collective-permute-start | bytes 983048 | tf_op jit(solution)/shard_map/ppermute | solution.py:237
  19.8 20.6 %collective-permute-start.26 = (bf16[5,128,128]{2,1,0:T(8,128)(2,1)S(1)}, bf16[5,128,128]{2,1,0:T(8,128)(2,1)}, u32[]{:S(2)}, u32[]{:S(2)}) collective-permute-start(bf16[5,128,128]{2,1,0:T(8,128)(2,1)S(1)} %get-tuple-element.38), channel_id=1, source_target_pairs={{11,32},{9,33},{5,34},{8,35},{0,36},{13,37},{2,38},{7,39},{15,40},... | collective-permute-start | bytes 491528 | tf_op jit(solution)/shard_map/ppermute | solution.py:296
  23.3 19.9 %collective-permute-start.27 = (bf16[5,128,128]{2,1,0:T(8,128)(2,1)S(1)}, bf16[5,128,128]{2,1,0:T(8,128)(2,1)}, u32[]{:S(2)}, u32[]{:S(2)}) collective-permute-start(bf16[5,128,128]{2,1,0:T(8,128)(2,1)S(1)} %get-tuple-element.39), channel_id=1, source_target_pairs={{11,64},{9,65},{5,66},{8,67},{0,68},{13,69},{2,70},{7,71},{15,72},... | collective-permute-start | bytes 491528 | tf_op jit(solution)/shard_map/ppermute | solution.py:296
  33.7 14.3 %collective-permute-start.28 = (bf16[5,128,128]{2,1,0:T(8,128)(2,1)S(1)}, bf16[5,128,128]{2,1,0:T(8,128)(2,1)}, u32[]{:S(2)}, u32[]{:S(2)}) collective-permute-start(bf16[5,128,128]{2,1,0:T(8,128)(2,1)S(1)} %get-tuple-element.40), channel_id=1, source_target_pairs={{11,96},{9,97},{5,98},{8,99},{0,100},{13,101},{2,102},{7,103},{15,... | collective-permute-start | bytes 491528 | tf_op jit(solution)/shard_map/ppermute | solution.py:296
  33.7 25.2 %collective-permute-start.29 = (bf16[5,128,128]{2,1,0:T(8,128)(2,1)S(1)}, bf16[5,128,128]{2,1,0:T(8,128)(2,1)}, u32[]{:S(2)}, u32[]{:S(2)}) collective-permute-start(bf16[5,128,128]{2,1,0:T(8,128)(2,1)S(1)} %get-tuple-element.41), channel_id=1, source_target_pairs={{3,0},{14,1},{9,2},{11,3},{8,4},{6,5},{5,6},{0,7},{7,8},{2,9},{13,... | collective-permute-start | bytes 491528 | tf_op jit(solution)/shard_map/ppermute | solution.py:296
  35.6 23.3 %collective-permute-start.30 = (bf16[5,128,128]{2,1,0:T(8,128)(2,1)S(1)}, bf16[5,128,128]{2,1,0:T(8,128)(2,1)}, u32[]{:S(2)}, u32[]{:S(2)}) collective-permute-start(bf16[5,128,128]{2,1,0:T(8,128)(2,1)S(1)} %get-tuple-element.42), channel_id=1, source_target_pairs={{3,32},{14,33},{9,34},{11,35},{8,36},{6,37},{5,38},{0,39},{7,40},{... | collective-permute-start | bytes 491528 | tf_op jit(solution)/shard_map/ppermute | solution.py:296
  40.4 61.0 %copy-start.3 = (bf16[64,2560]{0,1:T(8,128)(2,1)}, bf16[64,2560]{0,1:T(8,128)(2,1)S(1)}, u32[]{:S(2)}) copy-start(bf16[64,2560]{0,1:T(8,128)(2,1)S(1)} %copy.41) | copy-start | bytes 983044
  40.4 20.8 %collective-permute-start.31 = (bf16[5,128,128]{2,1,0:T(8,128)(2,1)S(1)}, bf16[5,128,128]{2,1,0:T(8,128)(2,1)S(1)}, u32[]{:S(2)}, u32[]{:S(2)}) collective-permute-start(bf16[5,128,128]{2,1,0:T(8,128)(2,1)S(1)} %get-tuple-element.43), channel_id=1, source_target_pairs={{3,64},{14,65},{9,66},{11,67},{8,68},{6,69},{5,70},{0,71},{7,72},{... | collective-permute-start | bytes 491528 | tf_op jit(solution)/shard_map/ppermute | solution.py:296
  43.2 18.0 %collective-permute-start.32 = (bf16[5,128,128]{2,1,0:T(8,128)(2,1)S(1)}, bf16[5,128,128]{2,1,0:T(8,128)(2,1)S(1)}, u32[]{:S(2)}, u32[]{:S(2)}) collective-permute-start(bf16[5,128,128]{2,1,0:T(8,128)(2,1)S(1)} %get-tuple-element.44), channel_id=1, source_target_pairs={{3,96},{14,97},{9,98},{11,99},{8,100},{6,101},{5,102},{0,103},{7,1... | collective-permute-start | bytes 491528 | tf_op jit(solution)/shard_map/ppermute | solution.py:296
  47.9 21.5 %collective-permute-start.5 = (bf16[5,128,128]{2,1,0:T(8,128)(2,1)S(1)}, bf16[5,128,128]{2,1,0:T(8,128)(2,1)S(1)}, u32[]{:S(2)}, u32[]{:S(2)}) collective-permute-start(bf16[5,128,128]{2,1,0:T(8,128)(2,1)S(1)} %get-tuple-element.29), channel_id=1, source_target_pairs={{12,0},{6,1},{1,2},{0,3},{3,4},{14,5},{10,6},{11,7},{8,8},{13,9},{... | collective-permute-start | bytes 491528 | tf_op jit(solution)/shard_map/ppermute | solution.py:296
  58.9 15.0 %collective-permute-start.6 = (bf16[5,128,128]{2,1,0:T(8,128)(2,1)S(1)}, bf16[5,128,128]{2,1,0:T(8,128)(2,1)S(1)}, u32[]{:S(2)}, u32[]{:S(2)}) collective-permute-start(bf16[5,128,128]{2,1,0:T(8,128)(2,1)S(1)} %get-tuple-element.30), channel_id=1, source_target_pairs={{12,32},{6,33},{1,34},{0,35},{3,36},{14,37},{10,38},{11,39},{8,40}... | collective-permute-start | bytes 491528 | tf_op jit(solution)/shard_map/ppermute | solution.py:296
  58.9 15.0 %collective-permute-start.7 = (bf16[5,128,128]{2,1,0:T(8,128)(2,1)S(1)}, bf16[5,128,128]{2,1,0:T(8,128)(2,1)S(1)}, u32[]{:S(2)}, u32[]{:S(2)}) collective-permute-start(bf16[5,128,128]{2,1,0:T(8,128)(2,1)S(1)} %get-tuple-element.31), channel_id=1, source_target_pairs={{12,64},{6,65},{1,66},{0,67},{3,68},{14,69},{10,70},{11,71},{8,72}... | collective-permute-start | bytes 491528 | tf_op jit(solution)/shard_map/ppermute | solution.py:296
  61.2 28.5 %collective-permute-start.18 = (bf16[128,1280]{1,0:T(8,128)(2,1)S(1)}, bf16[128,1280]{1,0:T(8,128)(2,1)S(1)}, u32[]{:S(2)}, u32[]{:S(2)}) collective-permute-start(bf16[128,1280]{1,0:T(8,128)(2,1)S(1)} %copy-done.4), channel_id=1, source_target_pairs={{0,32},{1,33},{2,34},{3,35},{4,36},{5,37},{6,38},{7,39},{8,40},{9,... | collective-permute-start | bytes 983048 | tf_op jit(solution)/shard_map/ppermute | solution.py:237
  61.2 33.5 %collective-permute-start.13 = (bf16[128,2560]{0,1:T(8,128)(2,1)}, bf16[128,2560]{0,1:T(8,128)(2,1)}, u32[]{:S(2)}, u32[]{:S(2)}) collective-permute-start(bf16[128,2560]{0,1:T(8,128)(2,1)} %pad_maximum_fusion.5), channel_id=1, source_target_pairs={{0,3},{1,2},{2,1},{3,0},{4,7},{5,6},{6,5},{7,4},{8,11},{9,10},{10,... | collective-permute-start | bytes 1966088 | tf_op jit(solution)/shard_map/ppermute | solution.py:237
  65.5 29.0 %copy-start.21 = (s32[2,80]{1,0:T(2,128)S(1)}, s32[2,80]{1,0:T(2,128)}, u32[]{:S(2)}) copy-start(s32[2,80]{1,0:T(2,128)} %param.12) | copy-start | bytes 1924
  65.5 36.0 %copy-start.2 = (bf16[2560,64]{1,0:T(8,128)(2,1)S(1)}, bf16[2560,64]{1,0:T(8,128)(2,1)}, u32[]{:S(2)}) copy-start(bf16[2560,64]{1,0:T(8,128)(2,1)} %copy.37) | copy-start | bytes 983044
  69.4 10.1 %collective-permute-start.8 = (bf16[5,128,128]{2,1,0:T(8,128)(2,1)S(1)}, bf16[5,128,128]{2,1,0:T(8,128)(2,1)S(1)}, u32[]{:S(2)}, u32[]{:S(2)}) collective-permute-start(bf16[5,128,128]{2,1,0:T(8,128)(2,1)S(1)} %get-tuple-element.32), channel_id=1, source_target_pairs={{12,96},{6,97},{1,98},{0,99},{3,100},{14,101},{10,102},{11,103},{8... | collective-permute-start | bytes 491528 | tf_op jit(solution)/shard_map/ppermute | solution.py:296
  73.9 20.4 %copy-start.13 = (bf16[5,128,128]{2,1,0:T(8,128)(2,1)}, bf16[5,128,128]{2,1,0:T(8,128)(2,1)S(1)}, u32[]{:S(2)}) copy-start(bf16[5,128,128]{2,1,0:T(8,128)(2,1)S(1)} %collective-permute-done.6) | copy-start | bytes 491524
  73.9 11.7 %collective-permute-start.1 = (bf16[5,128,128]{2,1,0:T(8,128)(2,1)S(1)}, bf16[5,128,128]{2,1,0:T(8,128)(2,1)S(1)}, u32[]{:S(2)}, u32[]{:S(2)}) collective-permute-start(bf16[5,128,128]{2,1,0:T(8,128)(2,1)S(1)} %get-tuple-element.26), channel_id=1, source_target_pairs={{4,32},{1,33},{14,34},{3,35},{11,36},{2,37},{13,38},{8,39},{0,40},... | collective-permute-start | bytes 491528 | tf_op jit(solution)/shard_map/ppermute | solution.py:296
  73.9 20.6 %copy-start.14 = (bf16[5,128,128]{2,1,0:T(8,128)(2,1)}, bf16[5,128,128]{2,1,0:T(8,128)(2,1)S(1)}, u32[]{:S(2)}) copy-start(bf16[5,128,128]{2,1,0:T(8,128)(2,1)S(1)} %collective-permute-done.7) | copy-start | bytes 491524
  73.9 15.7 %collective-permute-start.2 = (bf16[5,128,128]{2,1,0:T(8,128)(2,1)S(1)}, bf16[5,128,128]{2,1,0:T(8,128)(2,1)S(1)}, u32[]{:S(2)}, u32[]{:S(2)}) collective-permute-start(bf16[5,128,128]{2,1,0:T(8,128)(2,1)S(1)} %get-tuple-element.27), channel_id=1, source_target_pairs={{4,64},{1,65},{14,66},{3,67},{11,68},{2,69},{13,70},{8,71},{0,72},... | collective-permute-start | bytes 491528 | tf_op jit(solution)/shard_map/ppermute | solution.py:296
  79.5 57.2 %copy-start.15 = (bf16[5,128,128]{2,1,0:T(8,128)(2,1)}, bf16[5,128,128]{2,1,0:T(8,128)(2,1)S(1)}, u32[]{:S(2)}) copy-start(bf16[5,128,128]{2,1,0:T(8,128)(2,1)S(1)} %collective-permute-done.8) | copy-start | bytes 491524
  79.5 12.6 %collective-permute-start.3 = (bf16[5,128,128]{2,1,0:T(8,128)(2,1)S(1)}, bf16[5,128,128]{2,1,0:T(8,128)(2,1)S(1)}, u32[]{:S(2)}, u32[]{:S(2)}) collective-permute-start(bf16[5,128,128]{2,1,0:T(8,128)(2,1)S(1)} %get-tuple-element.28), channel_id=1, source_target_pairs={{4,96},{1,97},{14,98},{3,99},{11,100},{2,101},{13,102},{8,103},{0,... | collective-permute-start | bytes 491528 | tf_op jit(solution)/shard_map/ppermute | solution.py:296
  85.6 51.1 %copy-start.16 = (bf16[5,128,128]{2,1,0:T(8,128)(2,1)}, bf16[5,128,128]{2,1,0:T(8,128)(2,1)S(1)}, u32[]{:S(2)}) copy-start(bf16[5,128,128]{2,1,0:T(8,128)(2,1)S(1)} %collective-permute-done.1) | copy-start | bytes 491524
  85.6 8.7 %collective-permute-start = (bf16[5,128,128]{2,1,0:T(8,128)(2,1)S(1)}, bf16[5,128,128]{2,1,0:T(8,128)(2,1)}, u32[]{:S(2)}, u32[]{:S(2)}) collective-permute-start(bf16[5,128,128]{2,1,0:T(8,128)(2,1)S(1)} %get-tuple-element.25), channel_id=1, source_target_pairs={{4,0},{1,1},{14,2},{3,3},{11,4},{2,5},{13,6},{8,7},{0,8},{5,9},{10... | collective-permute-start | bytes 491528 | tf_op jit(solution)/shard_map/ppermute | solution.py:296
  89.6 47.1 %copy-start.17 = (bf16[5,128,128]{2,1,0:T(8,128)(2,1)}, bf16[5,128,128]{2,1,0:T(8,128)(2,1)S(1)}, u32[]{:S(2)}) copy-start(bf16[5,128,128]{2,1,0:T(8,128)(2,1)S(1)} %collective-permute-done.2) | copy-start | bytes 491524
  89.6 14.5 %collective-permute-start.33 = (bf16[2,2,5,128,128]{4,3,2,1,0:T(8,128)(2,1)}, bf16[2,2,5,128,128]{4,3,2,1,0:T(8,128)(2,1)}, u32[]{:S(2)}, u32[]{:S(2)}) collective-permute-start(bf16[2,2,5,128,128]{4,3,2,1,0:T(8,128)(2,1)} %bitcast.31.refs_4_), channel_id=1, source_target_pairs={{0,1},{1,0},{2,3},{3,2},{4,5},{5,4},{6,7},{7,6},{8,9},{9,8},{10,11... | collective-permute-start | bytes 1966088 | tf_op jit(solution)/shard_map/ppermute | solution.py:237
  89.7 47.0 %copy-start.5 = (bf16[128,1280]{1,0:T(8,128)(2,1)}, bf16[128,1280]{1,0:T(8,128)(2,1)S(1)}, u32[]{:S(2)}) copy-start(bf16[128,1280]{1,0:T(8,128)(2,1)S(1)} %collective-permute-done.18) | copy-start | bytes 983044
  89.7 27.2 %collective-permute-start.34 = (bf16[2,2,5,128,128]{4,3,2,1,0:T(8,128)(2,1)}, bf16[2,2,5,128,128]{4,3,2,1,0:T(8,128)(2,1)}, u32[]{:S(2)}, u32[]{:S(2)}) collective-permute-start(bf16[2,2,5,128,128]{4,3,2,1,0:T(8,128)(2,1)} %bitcast.36.refs_5_), channel_id=1, source_target_pairs={{0,1},{1,0},{2,3},{3,2},{4,5},{5,4},{6,7},{7,6},{8,9},{9,8},{10,11... | collective-permute-start | bytes 1966088 | tf_op jit(solution)/shard_map/ppermute | solution.py:237
  92.1 24.9 %copy-start.19 = (bf16[5,128,128]{2,1,0:T(8,128)(2,1)}, bf16[5,128,128]{2,1,0:T(8,128)(2,1)S(1)}, u32[]{:S(2)}) copy-start(bf16[5,128,128]{2,1,0:T(8,128)(2,1)S(1)} %collective-permute-done.3) | copy-start | bytes 491524
  92.1 38.9 %collective-permute-start.35 = (bf16[2,2,5,128,128]{4,3,2,1,0:T(8,128)(2,1)}, bf16[2,2,5,128,128]{4,3,2,1,0:T(8,128)(2,1)}, u32[]{:S(2)}, u32[]{:S(2)}) collective-permute-start(bf16[2,2,5,128,128]{4,3,2,1,0:T(8,128)(2,1)} %bitcast.41.refs_6_), channel_id=1, source_target_pairs={{0,1},{1,0},{2,3},{3,2},{4,5},{5,4},{6,7},{7,6},{8,9},{9,8},{10,11... | collective-permute-start | bytes 1966088 | tf_op jit(solution)/shard_map/ppermute | solution.py:237
  94.3 41.0 %collective-permute-start.19 = (bf16[256,1280]{1,0:T(8,128)(2,1)}, bf16[256,1280]{1,0:T(8,128)(2,1)S(1)}, u32[]{:S(2)}, u32[]{:S(2)}) collective-permute-start(bf16[256,1280]{1,0:T(8,128)(2,1)} %pad_maximum_fusion.6), channel_id=1, source_target_pairs={{0,96},{1,97},{2,98},{3,99},{4,100},{5,101},{6,102},{7,103},{8,104... | collective-permute-start | bytes 1966088 | tf_op jit(solution)/shard_map/ppermute | solution.py:237
  94.8 41.9 %collective-permute-start.36 = (bf16[2,2,5,128,128]{4,3,2,1,0:T(8,128)(2,1)}, bf16[2,2,5,128,128]{4,3,2,1,0:T(8,128)(2,1)S(1)}, u32[]{:S(2)}, u32[]{:S(2)}) collective-permute-start(bf16[2,2,5,128,128]{4,3,2,1,0:T(8,128)(2,1)} %bitcast.31.refs_4_), channel_id=1, source_target_pairs={{0,16},{1,17},{2,18},{3,19},{4,20},{5,21},{6,22},{7,23},{8,24},{9,... | collective-permute-start | bytes 1966088 | tf_op jit(solution)/shard_map/ppermute | solution.py:237
  104.2 37.7 %collective-permute-start.14 = (bf16[256,2560]{0,1:T(8,128)(2,1)}, bf16[256,2560]{0,1:T(8,128)(2,1)}, u32[]{:S(2)}, u32[]{:S(2)}) collective-permute-start(bf16[256,2560]{0,1:T(8,128)(2,1)} %pad_maximum_fusion.1), channel_id=1, source_target_pairs={{0,4},{1,5},{2,6},{3,7},{4,0},{5,1},{6,2},{7,3},{8,12},{9,13},{10,... | collective-permute-start | bytes 3932168 | tf_op jit(solution)/shard_map/ppermute | solution.py:237
  117.0 25.0 %collective-permute-start.16 = (bf16[256,2560]{0,1:T(8,128)(2,1)}, bf16[256,2560]{0,1:T(8,128)(2,1)}, u32[]{:S(2)}, u32[]{:S(2)}) collective-permute-start(bf16[256,2560]{0,1:T(8,128)(2,1)} %pad_maximum_fusion.1), channel_id=1, source_target_pairs={{0,12},{1,13},{2,14},{3,15},{4,8},{5,9},{6,10},{7,11},{8,4},{9,5},... | collective-permute-start | bytes 3932168 | tf_op jit(solution)/shard_map/ppermute | solution.py:237
  131.0 10.1 %collective-permute-start.37 = (bf16[2,2,5,128,128]{4,3,2,1,0:T(8,128)(2,1)}, bf16[2,2,5,128,128]{4,3,2,1,0:T(8,128)(2,1)S(1)}, u32[]{:S(2)}, u32[]{:S(2)}) collective-permute-start(bf16[2,2,5,128,128]{4,3,2,1,0:T(8,128)(2,1)} %bitcast.36.refs_5_), channel_id=1, source_target_pairs={{0,16},{1,17},{2,18},{3,19},{4,20},{5,21},{6,22},{7,23},{8,24},{9,... | collective-permute-start | bytes 1966088 | tf_op jit(solution)/shard_map/ppermute | solution.py:237
  135.3 5.8 %copy-start.6 = (bf16[256,1280]{1,0:T(8,128)(2,1)}, bf16[256,1280]{1,0:T(8,128)(2,1)S(1)}, u32[]{:S(2)}) copy-start(bf16[256,1280]{1,0:T(8,128)(2,1)S(1)} %collective-permute-done.19) | copy-start | bytes 1966084
  135.3 6.2 %collective-permute-start.38 = (bf16[2,2,5,128,128]{4,3,2,1,0:T(8,128)(2,1)}, bf16[2,2,5,128,128]{4,3,2,1,0:T(8,128)(2,1)}, u32[]{:S(2)}, u32[]{:S(2)}) collective-permute-start(bf16[2,2,5,128,128]{4,3,2,1,0:T(8,128)(2,1)} %bitcast.41.refs_6_), channel_id=1, source_target_pairs={{0,16},{1,17},{2,18},{3,19},{4,20},{5,21},{6,22},{7,23},{8,24},{9,... | collective-permute-start | bytes 1966088 | tf_op jit(solution)/shard_map/ppermute | solution.py:237
  137.6 35.5 %collective-permute-start.20 = (bf16[512,1280]{1,0:T(8,128)(2,1)}, bf16[512,1280]{1,0:T(8,128)(2,1)}, u32[]{:S(2)}, u32[]{:S(2)}) collective-permute-start(bf16[512,1280]{1,0:T(8,128)(2,1)} %pad_maximum_fusion.2), channel_id=1, source_target_pairs={{0,16},{1,17},{2,18},{3,19},{4,20},{5,21},{6,22},{7,23},{8,24},{9,... | collective-permute-start | bytes 3932168 | tf_op jit(solution)/shard_map/ppermute | solution.py:237
  138.4 11.3 %copy-start.22 = (s32[2,80]{1,0:T(2,128)S(1)}, s32[2,80]{1,0:T(2,128)}, u32[]{:S(2)}) copy-start(s32[2,80]{1,0:T(2,128)} %param.11) | copy-start | bytes 1924
  139.6 33.5 %copy-start.7 = (bf16[4,5,128,128]{3,2,1,0:T(8,128)(2,1)}, bf16[4,5,128,128]{3,2,1,0:T(8,128)(2,1)S(1)}, u32[]{:S(2)}) copy-start(bf16[4,5,128,128]{3,2,1,0:T(8,128)(2,1)S(1)} %pad_maximum_fusion.4) | copy-start | bytes 1966084
  141.1 32.6 %copy-start.8 = (bf16[4,5,128,128]{3,2,1,0:T(8,128)(2,1)}, bf16[4,5,128,128]{3,2,1,0:T(8,128)(2,1)S(1)}, u32[]{:S(2)}) copy-start(bf16[4,5,128,128]{3,2,1,0:T(8,128)(2,1)S(1)} %pad_maximum_fusion.3) | copy-start | bytes 1966084
  141.1 0.9 copy-start.10
  141.1 6.5 %collective-permute-start.40 = (bf16[2,2,5,128,128]{4,3,2,1,0:T(8,128)(2,1)S(1)}, bf16[2,2,5,128,128]{4,3,2,1,0:T(8,128)(2,1)S(1)}, u32[]{:S(2)}, u32[]{:S(2)}) collective-permute-start(bf16[2,2,5,128,128]{4,3,2,1,0:T(8,128)(2,1)S(1)} %bitcast.54), channel_id=1, source_target_pairs={{0,16},{1,17},{2,18},{3,19},{4,20},{5,21},{6,22},{7,23},{8,24},{9,... | collective-permute-start | bytes 1966088 | tf_op jit(solution)/shard_map/ppermute | solution.py:237
  141.4 6.2 %collective-permute-start.39 = (bf16[2,2,5,128,128]{4,3,2,1,0:T(8,128)(2,1)S(1)}, bf16[2,2,5,128,128]{4,3,2,1,0:T(8,128)(2,1)S(1)}, u32[]{:S(2)}, u32[]{:S(2)}) collective-permute-start(bf16[2,2,5,128,128]{4,3,2,1,0:T(8,128)(2,1)S(1)} %bitcast.57), channel_id=1, source_target_pairs={{0,16},{1,17},{2,18},{3,19},{4,20},{5,21},{6,22},{7,23},{8,24},{9,... | collective-permute-start | bytes 1966088 | tf_op jit(solution)/shard_map/ppermute | solution.py:237
  141.8 16.1 %collective-permute-start.9 = (bf16[2,2,5,128,128]{4,3,2,1,0:T(8,128)(2,1)S(1)}, bf16[2,2,5,128,128]{4,3,2,1,0:T(8,128)(2,1)S(1)}, u32[]{:S(2)}, u32[]{:S(2)}) collective-permute-start(bf16[2,2,5,128,128]{4,3,2,1,0:T(8,128)(2,1)S(1)} %bitcast.55), channel_id=1, source_target_pairs={{0,1},{1,0},{2,3},{3,2},{4,5},{5,4},{6,7},{7,6},{8,9},{9,8},{10,11... | collective-permute-start | bytes 1966088 | tf_op jit(solution)/shard_map/ppermute | solution.py:237
  142.0 29.9 %collective-permute-start.4 = (bf16[2,2,5,128,128]{4,3,2,1,0:T(8,128)(2,1)S(1)}, bf16[2,2,5,128,128]{4,3,2,1,0:T(8,128)(2,1)S(1)}, u32[]{:S(2)}, u32[]{:S(2)}) collective-permute-start(bf16[2,2,5,128,128]{4,3,2,1,0:T(8,128)(2,1)S(1)} %bitcast.58), channel_id=1, source_target_pairs={{0,1},{1,0},{2,3},{3,2},{4,5},{5,4},{6,7},{7,6},{8,9},{9,8},{10,11... | collective-permute-start | bytes 1966088 | tf_op jit(solution)/shard_map/ppermute | solution.py:237
  147.6 25.4 %collective-permute-start.15 = (bf16[128,2560]{0,1:T(8,128)(2,1)}, bf16[128,2560]{0,1:T(8,128)(2,1)}, u32[]{:S(2)}, u32[]{:S(2)}) collective-permute-start(bf16[128,2560]{0,1:T(8,128)(2,1)} %slice.20), channel_id=1, source_target_pairs={{0,12},{1,13},{2,14},{3,15},{4,8},{5,9},{6,10},{7,11},{8,4},{9,5},... | collective-permute-start | bytes 1966088 | tf_op jit(solution)/shard_map/ppermute | solution.py:237
  148.5 25.2 %collective-permute-start.17 = (bf16[128,2560]{0,1:T(8,128)(2,1)}, bf16[128,2560]{0,1:T(8,128)(2,1)}, u32[]{:S(2)}, u32[]{:S(2)}) collective-permute-start(bf16[128,2560]{0,1:T(8,128)(2,1)} %slice.21), channel_id=1, source_target_pairs={{0,4},{1,5},{2,6},{3,7},{4,0},{5,1},{6,2},{7,3},{8,12},{9,13},{10,... | collective-permute-start | bytes 1966088 | tf_op jit(solution)/shard_map/ppermute | solution.py:237
  158.0 31.7 %collective-permute-start.41 = (bf16[2,2,5,128,128]{4,3,2,1,0:T(8,128)(2,1)}, bf16[2,2,5,128,128]{4,3,2,1,0:T(8,128)(2,1)}, u32[]{:S(2)}, u32[]{:S(2)}) collective-permute-start(bf16[2,2,5,128,128]{4,3,2,1,0:T(8,128)(2,1)} %collective-permute-done.33.refs_9_), channel_id=1, source_target_pairs={{0,16},{1,17},{2,18},{3,19},{4,20},{5,21},{6,22},{7,23},{8,24},{9,... | collective-permute-start | bytes 1966088 | tf_op jit(solution)/shard_map/ppermute | solution.py:237
  171.9 17.7 %collective-permute-start.42 = (bf16[2,2,5,128,128]{4,3,2,1,0:T(8,128)(2,1)}, bf16[2,2,5,128,128]{4,3,2,1,0:T(8,128)(2,1)}, u32[]{:S(2)}, u32[]{:S(2)}) collective-permute-start(bf16[2,2,5,128,128]{4,3,2,1,0:T(8,128)(2,1)} %collective-permute-done.34.refs_10_), channel_id=1, source_target_pairs={{0,16},{1,17},{2,18},{3,19},{4,20},{5,21},{6,22},{7,23},{8,24},{9,... | collective-permute-start | bytes 1966088 | tf_op jit(solution)/shard_map/ppermute | solution.py:237
  173.0 16.6 %collective-permute-start.43 = (bf16[2,2,5,128,128]{4,3,2,1,0:T(8,128)(2,1)}, bf16[2,2,5,128,128]{4,3,2,1,0:T(8,128)(2,1)}, u32[]{:S(2)}, u32[]{:S(2)}) collective-permute-start(bf16[2,2,5,128,128]{4,3,2,1,0:T(8,128)(2,1)} %collective-permute-done.35.refs_11_), channel_id=1, source_target_pairs={{0,16},{1,17},{2,18},{3,19},{4,20},{5,21},{6,22},{7,23},{8,24},{9,... | collective-permute-start | bytes 1966088 | tf_op jit(solution)/shard_map/ppermute | solution.py:237
  173.1 34.0 %collective-permute-start.11 = (bf16[2,2,5,128,128]{4,3,2,1,0:T(8,128)(2,1)S(1)}, bf16[2,2,5,128,128]{4,3,2,1,0:T(8,128)(2,1)S(1)}, u32[]{:S(2)}, u32[]{:S(2)}) collective-permute-start(bf16[2,2,5,128,128]{4,3,2,1,0:T(8,128)(2,1)S(1)} %collective-permute-done.9.refs_1_), channel_id=1, source_target_pairs={{0,16},{1,17},{2,18},{3,19},{4,20},{5,21},{6,22},{7,23},{8,24},{9,... | collective-permute-start | bytes 1966088 | tf_op jit(solution)/shard_map/ppermute | solution.py:237
  173.7 33.5 %collective-permute-start.10 = (bf16[2,2,5,128,128]{4,3,2,1,0:T(8,128)(2,1)S(1)}, bf16[2,2,5,128,128]{4,3,2,1,0:T(8,128)(2,1)S(1)}, u32[]{:S(2)}, u32[]{:S(2)}) collective-permute-start(bf16[2,2,5,128,128]{4,3,2,1,0:T(8,128)(2,1)S(1)} %collective-permute-done.4.refs_0_), channel_id=1, source_target_pairs={{0,16},{1,17},{2,18},{3,19},{4,20},{5,21},{6,22},{7,23},{8,24},{9,... | collective-permute-start | bytes 1966088 | tf_op jit(solution)/shard_map/ppermute | solution.py:237
  189.7 17.5 %copy-start.1 = (s32[74]{0:T(128)S(1)}, s32[74]{0:T(128)}, u32[]{:S(2)}) copy-start(s32[74]{0:T(128)} %concatenate.33.refs_0_.scal) | copy-start | bytes 892
  (4 other events, 3.2 us)
where the time goes:
time: 215 us; the launch traced here: 214 us
  starting transfers between devices  82 us (38%)
  waiting for transfers between devices  57.1 us (27%)
  local copies, waits for them, and re-layouts  29.5 us (14%)
  Pallas kernels  25.6 us (12%)
  other arithmetic  19.3 us (9%)
    ppermute x20, starting transfers between devices, compute(): got.append(lax.ppermute(packed[r * XS + g], ('row', 'col'), route))  54.3 us
    ppermute x24, waiting for transfers between devices, hop(): return lax.ppermute(array, ('row', 'col'), route)  44.1 us
    ppermute x24, starting transfers between devices, hop(): return lax.ppermute(array, ('row', 'col'), route)  27.7 us
    pallas_call x1, Pallas kernels, base(): pl.pallas_call(kernel, grid_spec=spec, out_shape=jax.ShapeDtypeStruct((PR...  17.4 us
    ppermute x20, waiting for transfers between devices, compute(): got.append(lax.ppermute(packed[r * XS + g], ('row', 'col'), route))  13 us
    concatenate x1, local copies, waits for them, and re-layouts, compute(): lower_all = jnp.concatenate([low_here, low_y1, low_y2a, low_y2b, low_y3]).T  8.99 us
    another operation x5, other arithmetic, compute(): held.append(jnp.stack(got).reshape(2, 2, KR, TILE, TILE))  8.73 us
    unnamed x49, local copies, waits for them, and re-layouts  7.32 us
  transfers between devices with their start and end apart: 44, of which 7 were waited for; matrix products, arithmetic and copies ran while one was open for 20% of the time, Pallas kernels for 8%

commit v1 on v0

--- a/solution.py
+++ b/solution.py
@@ -71,10 +71,10 @@
 
 def pack_kernel(where, children, *outs):
     for r in range(ROUNDS):
-        start = pl.multiple_of(where[XS + r] * TILE, TILE)
-        for g in range(XS):
+        start = pl.multiple_of(where[r] * TILE, TILE)
+        for x in range(XS):
             for kk in range(KR):
-                outs[r * XS + g][kk] = children[kk, where[g], :, pl.ds(start, TILE)]
+                outs[r][x, kk] = children[kk, x, :, pl.ds(start, TILE)]
 
 
 def pack(children, where):
@@ -82,47 +82,46 @@
         num_scalar_prefetch=1,
         grid=(1,),
         in_specs=[pl.BlockSpec((KR, XS, TILE, KC * TILE), lambda i, w: (0, 0, 0, 0))],
-        out_specs=[pl.BlockSpec((KR, TILE, TILE), lambda i, w: (0, 0, 0))] * (ROUNDS * XS),
+        out_specs=[pl.BlockSpec((XS, KR, TILE, TILE), lambda i, w: (0, 0, 0, 0))] * ROUNDS,
     )
     return pl.pallas_call(
         pack_kernel,
         grid_spec=spec,
-        out_shape=[jax.ShapeDtypeStruct((KR, TILE, TILE), jnp.bfloat16)] * (ROUNDS * XS),
+        out_shape=[jax.ShapeDtypeStruct((XS, KR, TILE, TILE), jnp.bfloat16)] * ROUNDS,
         compiler_params=pltpu.CompilerParams(vmem_limit_bytes=32 << 20),
         cost_estimate=pl.CostEstimate(flops=0, bytes_accessed=6553600, transcendentals=0),
         name="pack",
     )(where, children.reshape(KR, XS, TILE, KC * TILE))
 
 
-CORE, X_LO, X_HI, SLOT, COL_ON, ROW_ON = 0, 1, 2, 4, 14, 34
+CORE, SLOT, COL_ON, ROW_ON = 0, 1, 11, 31
 UNIT = (2, 1, KR, TILE, TILE)
 HEIGHT = KR * TILE
 
 
-def half_of(matches, block, scal):
-    return jnp.where(matches, block // 2, jnp.maximum(block - 1, 0) // 2) ^ scal[X_LO]
+def half_of(matches, block):
+    return jnp.where(matches, block // 2, jnp.maximum(block - 1, 0) // 2)
 
 
 def own_map(b, s):
-    return (0, half_of(s[CORE] == b % 2, b, s), 0, 0, 0)
+    return (0, half_of(s[CORE] == b % 2, b), 0, 0, 0)
 
 
 def other_map(b, s):
-    return (0, half_of(s[CORE] != b % 2, b, s), 0, 0, 0)
+    return (0, half_of(s[CORE] != b % 2, b), 0, 0, 0)
 
 
 def add_unit(scal, spot, block, unit, out, start):
-    for g in range(2):
-        child = g ^ scal[X_HI]
-
-        @pl.when(scal[COL_ON + spot * 2 + g] == 1)
+    for child in range(2):
+
+        @pl.when(scal[COL_ON + spot * 2 + child] == 1)
         def _():
             for kk in range(KR):
 
                 @pl.when(scal[ROW_ON + child * PRB + block * KR + kk] == 1)
                 def _():
                     rows = pl.ds(kk * TILE, TILE)
-                    out[rows, pl.ds(start, TILE)] += unit[g, 0, kk].astype(jnp.float32)
+                    out[rows, pl.ds(start, TILE)] += unit[child, 0, kk].astype(jnp.float32)
 
 
 def base_kernel(spots, scal, listed, lower, upper, *refs):
@@ -251,50 +250,28 @@
             tile_of[r, j // KC] = j % KC
             slot_of[r, target] = j // 8
 
-    low = lower_panel.T
-    low_z1 = hop(low, col_mask=1)
-    low01 = jnp.concatenate([low, low_z1])
-    low32 = hop(low01, col_mask=3)
-    low_here = jnp.concatenate([low01, low32])
-    low_y1 = hop(low_here, col_mask=4)
-    low_y3 = hop(low_here, col_mask=12)
-    low_y2a = hop(low_y1[:128], col_mask=12)
-    low_y2b = hop(low_y3[128:], col_mask=4)
-    lower_all = jnp.concatenate([low_here, low_y1, low_y2a, low_y2b, low_y3]).T
-    piece_col = col ^ (
-        4 * jnp.asarray([0, 1, 2, 3], jnp.int32)[:, None]
-        + jnp.asarray([0, 1, 3, 2], jnp.int32)[None, :]
-    ).reshape(-1)
-
-    up_x1 = hop(upper_panel, row_mask=2)
-    up01 = jnp.concatenate([upper_panel, up_x1])
-    up32 = hop(up01, row_mask=6)
-    up_here = jnp.concatenate([up01, up32])
-    up_core = hop(up_here, row_mask=1)
-    up_pieces = jnp.concatenate([up_here, up_core]).reshape(2, XS, 2, 64, PC * TILE)
-    piece_row = row ^ (piece_col >> 1)
-    flip = piece_row >> 1
-    place = jnp.where(flip == 2, 3, jnp.where(flip == 3, 2, flip))
-    index = ((piece_row & 1) * XS + place) * 2 + (piece_col & 1)
-    upper_all = jnp.take(up_pieces.reshape(16, 64, PC * TILE), index, axis=0, mode="clip")
-    upper_all = upper_all.reshape(1024, PC * TILE)
-
-    where = jnp.concatenate(
-        [chip ^ jnp.arange(XS, dtype=jnp.int32), jnp.asarray(tile_of)[:, col]]
-    ).astype(jnp.int32)
-    packed = pack(children, where)
+    along_z = [[4 * y + z for z in range(4)] for y in range(4)]
+    along_y = [[4 * y + z for y in range(4)] for z in range(4)]
+    lower_here = lax.all_gather(
+        lower_panel.T, "col", axis=0, tiled=True, axis_index_groups=along_z
+    )
+    upper_all = lax.all_gather(upper_panel, "row", axis=0, tiled=True)
+
+    packed = pack(children, jnp.asarray(tile_of)[:, col])
 
     held, swapped, core_held, core_swapped = [], [], [], []
+    same_core = [[2 * x + c for x in range(XS)] for c in range(2)]
     for r in range(ROUNDS):
-        got = []
-        for g in range(XS):
-            route = [
-                (p * COLS + source_of[r][q], (p ^ (2 * g)) * COLS + q)
-                for p in range(ROWS)
-                for q in range(COLS)
-            ]
-            got.append(lax.ppermute(packed[r * XS + g], ("row", "col"), route))
-        held.append(jnp.stack(got).reshape(2, 2, KR, TILE, TILE))
+        got = lax.all_to_all(
+            packed[r], "row", 0, 0, axis_index_groups=same_core, tiled=True
+        )
+        if r == 1:
+            lower_here, got = lax.optimization_barrier((lower_here, got))
+            lower_all = lax.all_gather(
+                lower_here, "col", axis=0, tiled=True, axis_index_groups=along_y
+            ).T
+        got = lax.ppermute(got, "col", [(source_of[r][q], q) for q in range(COLS)])
+        held.append(got.reshape(UNIT[0], 2, KR, TILE, TILE))
     for r in range(ROUNDS):
         swapped.append(hop(held[r], col_mask=1))
         core_held.append(hop(held[r], row_mask=1))
@@ -307,13 +284,12 @@
     col_on = lax.dynamic_slice_in_dim(col_maps.reshape(2, PC, 8), col >> 1, 1, 2)[:, :, 0]
     col_on = (col_on == col * PC + spots).astype(jnp.int32)
     slot = jnp.concatenate([jnp.asarray(slot_of)[:, col], jnp.asarray(slot_of)[:, col ^ 1]])
-    sides = (chip >> 1) ^ jnp.arange(2, dtype=jnp.int32)
     by_slot = jnp.sum(
-        jnp.where(slot[:, None] == spots[None, :], 1, 0)[:, None, :] * col_on[sides][None], axis=2
+        jnp.where(slot[:, None] == spots[None, :], 1, 0)[:, None, :] * col_on[None], axis=2
     )
     scal = jnp.concatenate(
         [
-            jnp.stack([core, chip & 1, chip >> 1, chip]),
+            core[None],
             slot,
             by_slot.reshape(-1),
             row_on.reshape(-1),

time: 215 us -> 255 us (1.19)
  the two profiles are of different devices: /device:TPU:49 before, /device:TPU:80 now
where the time goes in v1:
time: 255 us; the launch traced here: 250 us
  waiting for transfers between devices  97.3 us (38%)
  starting transfers between devices  56.2 us (22%)
  blocking collectives  46.7 us (18%)
  Pallas kernels  26.3 us (10%)
  between operations  13.4 us (5%)
  local copies, waits for them, and re-layouts  9.21 us (4%)
    ppermute x5, waiting for transfers between devices, compute(): got = lax.ppermute(got, 'col', [(source_of[r][q], q) for q in range(COLS)])  48.4 us
    all_to_all x3, blocking collectives, compute(): lax.all_to_all(packed[r], 'row', 0, 0, axis_index_groups=same_core, tiled...  46.7 us
    ppermute x5, starting transfers between devices, compute(): got = lax.ppermute(got, 'col', [(source_of[r][q], q) for q in range(COLS)])  32.4 us
    ppermute x15, waiting for transfers between devices, hop(): return lax.ppermute(array, ('row', 'col'), route)  27.6 us
    pallas_call x1, Pallas kernels, base(): pl.pallas_call(kernel, grid_spec=spec, out_shape=jax.ShapeDtypeStruct((PR...  17.5 us
    ppermute x15, starting transfers between devices, hop(): return lax.ppermute(array, ('row', 'col'), route)  16.7 us
    all_to_all x2, waiting for transfers between devices, compute(): lax.all_to_all(packed[r], 'row', 0, 0, axis_index_groups=same_core, tiled...  13.2 us
    all_to_all x2, starting transfers between devices, compute(): lax.all_to_all(packed[r], 'row', 0, 0, axis_index_groups=same_core, tiled...  6.97 us
  transfers between devices with their start and end apart: 25, of which 9 were waited for; matrix products, arithmetic and copies ran while one was open for 3% of the time, Pallas kernels for 8%

profile of v1, /device:TPU:80, one launch (start us, length us, event | category | flops | bytes accessed | tf_op | source)
XLA Modules:
  0.0 249.9 jit_solution(8701353839373989444)
XLA Ops:
  6.5 0.7 all-gather.4.cloned.1.call-update
  7.3 0.0 all-gather.8.cloned.1.call-start
  7.3 0.7 all-gather.8.cloned.1.call-update
  8.0 0.0 all-gather.6.cloned.1.call-start
  8.1 0.8 fusion.9
  8.8 1.9 copy-done
  10.8 2.1 pack.1
  12.8 15.0 %all_to_all.25 = bf16[4,5,128,128]{3,2,1,0:T(8,128)(2,1)S(1)} all-to-all(bf16[4,5,128,128]{3,2,1,0:T(8,128)(2,1)S(1)} %get-tuple-element.14), channel_id=1, replica_groups={{0,32,64,96},{16,48,80,112},{1,33,65,97},{17,49,81,113},{2,34,66,98},{1..., dimensions={0} | all-to-all | bytes 1310720 | tf_op jit(solution)/shard_map/all_to_all | solution.py:265
  27.8 6.7 %all-gather.4.cloned.1.call-done = bf16[256,2560]{1,0:T(8,128)(2,1)} async-done(((bf16[64,2560]{1,0:T(8,128)(2,1)}), bf16[256,2560]{1,0:T(8,128)(2,1)}) %all-gather.4.cloned.1.call-update) | async-done | bytes 1310736 | tf_op jit(solution)/shard_map/all_gather | solution.py:255
  34.5 2.4 copy.27
  36.9 0.0 all-gather.6.cloned.1.call-update
  36.9 13.9 %all_to_all.26 = bf16[4,5,128,128]{3,2,1,0:T(8,128)(2,1)S(1)} all-to-all(bf16[4,5,128,128]{3,2,1,0:T(8,128)(2,1)S(1)} %get-tuple-element.16), channel_id=1, replica_groups={{0,32,64,96},{16,48,80,112},{1,33,65,97},{17,49,81,113},{2,34,66,98},{1..., dimensions={0} | all-to-all | bytes 1310720 | tf_op jit(solution)/shard_map/all_to_all | solution.py:265
  50.8 17.8 %all_to_all.27 = bf16[4,5,128,128]{3,2,1,0:T(8,128)(2,1)S(1)} all-to-all(bf16[4,5,128,128]{3,2,1,0:T(8,128)(2,1)S(1)} %get-tuple-element.18), channel_id=1, replica_groups={{0,32,64,96},{16,48,80,112},{1,33,65,97},{17,49,81,113},{2,34,66,98},{1..., dimensions={0} | all-to-all | bytes 1310720 | tf_op jit(solution)/shard_map/all_to_all | solution.py:265
  68.7 3.5 %all-to-all-start = ((bf16[4,5,128,128]{3,2,1,0:T(8,128)(2,1)}), bf16[4,5,128,128]{3,2,1,0:T(8,128)(2,1)S(1)}, u32[]{:S(2)}, u32[]{:S(2)}) async-start(bf16[4,5,128,128]{3,2,1,0:T(8,128)(2,1)} %get-tuple-element.12), calls=%async_computation | async-start | bytes 1310720 | tf_op jit(solution)/shard_map/all_to_all | solution.py:265
  72.2 0.6 collective-permute-start.6
  72.7 9.4 %all-to-all-done = bf16[4,5,128,128]{3,2,1,0:T(8,128)(2,1)S(1)} async-done(((bf16[4,5,128,128]{3,2,1,0:T(8,128)(2,1)}), bf16[4,5,128,128]{3,2,1,0:T(8,128)(2,1)S(1)}, u32[]{:S(2)}, u32[]{:S(2)}) %all-to-all-start) | async-done | bytes 655392 | tf_op jit(solution)/shard_map/all_to_all | solution.py:265
  82.1 3.5 %all-to-all-start.1 = ((bf16[4,5,128,128]{3,2,1,0:T(8,128)(2,1)}), bf16[4,5,128,128]{3,2,1,0:T(8,128)(2,1)S(1)}, u32[]{:S(2)}, u32[]{:S(2)}) async-start(bf16[4,5,128,128]{3,2,1,0:T(8,128)(2,1)} %get-tuple-element.13), calls=%async_computation.1 | async-start | bytes 1310720 | tf_op jit(solution)/shard_map/all_to_all | solution.py:265
  85.6 3.5 %collective-permute-start.8 = (bf16[4,5,128,128]{3,2,1,0:T(8,128)(2,1)S(1)}, bf16[4,5,128,128]{3,2,1,0:T(8,128)(2,1)}, u32[]{:S(2)}, u32[]{:S(2)}) collective-permute-start(bf16[4,5,128,128]{3,2,1,0:T(8,128)(2,1)S(1)} %all_to_all.27), channel_id=1, source_target_pairs={{3,0},{14,1},{9,2},{11,3},{8,4},{6,5},{5,6},{0,7},{7,8},{2,9},{13,... | collective-permute-start | bytes 1966088 | tf_op jit(solution)/shard_map/ppermute | solution.py:273
  89.1 1.5 collective-permute-start
  90.6 3.8 %all-to-all-done.1 = bf16[4,5,128,128]{3,2,1,0:T(8,128)(2,1)S(1)} async-done(((bf16[4,5,128,128]{3,2,1,0:T(8,128)(2,1)}), bf16[4,5,128,128]{3,2,1,0:T(8,128)(2,1)S(1)}, u32[]{:S(2)}, u32[]{:S(2)}) %all-to-all-start.1) | async-done | bytes 655392 | tf_op jit(solution)/shard_map/all_to_all | solution.py:265
  94.4 2.4 collective-permute-start.2
  96.9 6.0 %collective-permute-start.9 = (bf16[2,2,5,128,128]{4,3,2,1,0:T(8,128)(2,1)}, bf16[2,2,5,128,128]{4,3,2,1,0:T(8,128)(2,1)S(1)}, u32[]{:S(2)}, u32[]{:S(2)}) collective-permute-start(bf16[2,2,5,128,128]{4,3,2,1,0:T(8,128)(2,1)} %bitcast.11.refs_4_), channel_id=1, source_target_pairs={{0,1},{1,0},{2,3},{3,2},{4,5},{5,4},{6,7},{7,6},{8,9},{9,8},{10,11... | collective-permute-start | bytes 1966088 | tf_op jit(solution)/shard_map/ppermute | solution.py:236
  102.9 0.0 collective-permute-start.12
  102.9 12.5 %collective-permute-done.8 = bf16[4,5,128,128]{3,2,1,0:T(8,128)(2,1)} collective-permute-done((bf16[4,5,128,128]{3,2,1,0:T(8,128)(2,1)S(1)}, bf16[4,5,128,128]{3,2,1,0:T(8,128)(2,1)}, u32[]{:S(2)}, u32[]{:S(2)}) %collective-permute-start.8) | collective-permute-done | bytes 655392 | tf_op jit(solution)/shard_map/ppermute | solution.py:273
  115.4 7.4 %collective-permute-start.11 = (bf16[2,2,5,128,128]{4,3,2,1,0:T(8,128)(2,1)}, bf16[2,2,5,128,128]{4,3,2,1,0:T(8,128)(2,1)}, u32[]{:S(2)}, u32[]{:S(2)}) collective-permute-start(bf16[2,2,5,128,128]{4,3,2,1,0:T(8,128)(2,1)} %bitcast.13.refs_6_), channel_id=1, source_target_pairs={{0,1},{1,0},{2,3},{3,2},{4,5},{5,4},{6,7},{7,6},{8,9},{9,8},{10,11... | collective-permute-start | bytes 1966088 | tf_op jit(solution)/shard_map/ppermute | solution.py:236
  122.8 0.0 collective-permute-start.14
  122.8 22.8 %collective-permute-done.2 = bf16[4,5,128,128]{3,2,1,0:T(8,128)(2,1)S(1)} collective-permute-done((bf16[4,5,128,128]{3,2,1,0:T(8,128)(2,1)S(1)}, bf16[4,5,128,128]{3,2,1,0:T(8,128)(2,1)S(1)}, u32[]{:S(2)}, u32[]{:S(2)}) %collective-permute-start.2) | collective-permute-done | bytes 655392 | tf_op jit(solution)/shard_map/ppermute | solution.py:273
  145.6 0.9 copy-done.2
  146.5 24.4 %collective-permute-start.7 = (bf16[4,5,128,128]{3,2,1,0:T(8,128)(2,1)S(1)}, bf16[4,5,128,128]{3,2,1,0:T(8,128)(2,1)}, u32[]{:S(2)}, u32[]{:S(2)}) collective-permute-start(bf16[4,5,128,128]{3,2,1,0:T(8,128)(2,1)S(1)} %all_to_all.25), channel_id=1, source_target_pairs={{11,0},{9,1},{5,2},{8,3},{0,4},{13,5},{2,6},{7,7},{15,8},{10,9},{1... | collective-permute-start | bytes 1966088 | tf_op jit(solution)/shard_map/ppermute | solution.py:273
  170.9 0.1 fusion.11
  170.9 0.1 reshape.80
  171.0 0.1 reshape.82
  171.1 0.2 dynamic-slice_reduce_fusion
  171.3 0.1 squeeze.18
  171.4 0.0 collective-permute-start.1
  171.4 0.0 collective-permute-done.12.refs_12_
  171.4 0.1 collective-permute-start.16
  171.5 13.1 %collective-permute-done.7 = bf16[4,5,128,128]{3,2,1,0:T(8,128)(2,1)} collective-permute-done((bf16[4,5,128,128]{3,2,1,0:T(8,128)(2,1)S(1)}, bf16[4,5,128,128]{3,2,1,0:T(8,128)(2,1)}, u32[]{:S(2)}, u32[]{:S(2)}) %collective-permute-start.7) | collective-permute-done | bytes 655392 | tf_op jit(solution)/shard_map/ppermute | solution.py:273
  184.7 0.1 eq.76
  184.8 0.2 dynamic-slice_reduce_fusion.1
  185.0 0.0 collective-permute-done.14.refs_14_
  185.0 2.1 collective-permute-start.3
  187.1 0.0 collective-permute-done.15.refs_15_
  187.1 0.0 collective-permute-start.17
  187.1 0.5 collective-permute-start.19
  187.6 1.4 collective-permute-done.1.refs_0_
  189.0 14.1 %collective-permute-done.10.refs_10_ = bf16[2,2,5,128,128]{4,3,2,1,0:T(8,128)(2,1)} collective-permute-done((bf16[2,2,5,128,128]{4,3,2,1,0:T(8,128)(2,1)}, bf16[2,2,5,128,128]{4,3,2,1,0:T(8,128)(2,1)}, u32[]{:S(2)}, u32[]{:S(2)}) %collective-permute-start.10) | collective-permute-done | bytes 655392 | tf_op jit(solution)/shard_map/ppermute | solution.py:236
  203.2 0.0 collective-permute-start.18
  203.2 0.1 pad_add_fusion
  203.3 0.1 fusion.7
  203.3 0.4 fusion
  203.7 12.0 %collective-permute-done.3.refs_1_ = bf16[2,2,5,128,128]{4,3,2,1,0:T(8,128)(2,1)S(1)} collective-permute-done((bf16[2,2,5,128,128]{4,3,2,1,0:T(8,128)(2,1)}, bf16[2,2,5,128,128]{4,3,2,1,0:T(8,128)(2,1)S(1)}, u32[]{:S(2)}, u32[]{:S(2)}) %collective-permute-start.3) | collective-permute-done | bytes 655392 | tf_op jit(solution)/shard_map/ppermute | solution.py:236
  215.7 0.0 collective-permute-start.4
  215.8 0.8 copy-done.6
  216.6 0.5 collective-permute-start.5
  217.1 0.2 multiply_reduce_fusion
  217.4 0.1 reshape.81
  217.4 0.1 broadcast_in_dim.25
  217.6 0.8 reshape_reshape.4.refs_1_
  218.3 0.7 concatenate.8.refs_0_.scal
  219.0 0.0 all-gather.8.cloned.1.call-done.refs_3_
  219.0 0.0 all-gather.6.cloned.1.call-done
  219.1 17.5 %base.1.refs_4_ = f32[2560,1280]{1,0:T(8,128)} custom-call(s32[71]{0:T(128)} %concatenate.8.refs_0_.scal, f32[20,1,1280]{2,1,0:T(1,128)} %reshape_reshape.4.refs_1_, bf16[2560,1024]{1,0:T(8,128)(2,1)} %bitcast.18, bf16[1024,1280]{1,0:T(8,128)(2,1)} %all-gather.8.cloned.1.call-done.refs_3_, bf16[2,2,5,128,128]{4,3,2,1,0:T(8,128)(2,1)} %bitcast.11.refs_4_, ...), custom_call_target="tpu_custom_call" | custom-call | flops 6710886400 | bytes 35651584 | tf_op jit(solution)/shard_map/base/pallas_call | solution.py:168
  236.6 6.8 %tail.1 = f32[2560,1280]{1,0:T(8,128)} custom-call(s32[71]{0:T(128)S(1)} %copy-done.1, bf16[2,2,5,128,128]{4,3,2,1,0:T(8,128)(2,1)S(1)} %collective-permute-done.1.refs_0_, bf16[2,2,5,128,128]{4,3,2,1,0:T(8,128)(2,1)S(1)} %collective-permute-done.3.refs_1_, ...), custom_call_target="tpu_custom_call", output_to_operand_aliasing={{}: (5, {})} | custom-call | bytes 8388608 | tf_op jit(solution)/shard_map/tail/pallas_call | solution.py:219
  (37 shorter events, 0.1 us)
Async XLA Ops:
  6.5 27.9 %all-gather.4.cloned.1.call-start = ((), (), s32[]{:S(2)}) async-start(), calls=%async_computation.5 | async-start | bytes 1638400 | tf_op jit(solution)/shard_map/all_gather | solution.py:255
  7.3 211.7 %all-gather.8.cloned.1.call-start = ((), (), s32[]{:S(2)}) async-start(), calls=%async_computation.7 | async-start | bytes 2949120 | tf_op jit(solution)/shard_map/all_gather | solution.py:258
  8.0 211.0 %all-gather.6.cloned.1.call-start = ((), (), s32[]{:S(2)}) async-start(), calls=%async_computation.6 | async-start | bytes 6553600 | tf_op jit(solution)/shard_map/all_gather | solution.py:270
  8.8 1.9 copy-start
  36.9 134.0 %copy-start.7 = (s32[8192,2]{0,1:T(2,128)S(1)}, s32[8192,2]{0,1:T(2,128)}, u32[]{:S(2)}) copy-start(s32[8192,2]{0,1:T(2,128)} %param.11) | copy-start | bytes 196612
  36.9 134.1 %copy-start.8 = (s32[2,80]{1,0:T(2,128)S(1)}, s32[2,80]{1,0:T(2,128)}, u32[]{:S(2)}) copy-start(s32[2,80]{1,0:T(2,128)} %param.10) | copy-start | bytes 1924
  36.9 134.1 %copy-start.9 = (s32[2,80]{1,0:T(2,128)S(1)}, s32[2,80]{1,0:T(2,128)}, u32[]{:S(2)}) copy-start(s32[2,80]{1,0:T(2,128)} %param.9) | copy-start | bytes 1924
  68.7 13.4 %all-to-all-start = ((bf16[4,5,128,128]{3,2,1,0:T(8,128)(2,1)}), bf16[4,5,128,128]{3,2,1,0:T(8,128)(2,1)S(1)}, u32[]{:S(2)}, u32[]{:S(2)}) async-start(bf16[4,5,128,128]{3,2,1,0:T(8,128)(2,1)} %get-tuple-element.12), calls=%async_computation | async-start | bytes 1310720 | tf_op jit(solution)/shard_map/all_to_all | solution.py:265
  72.2 24.7 %collective-permute-start.6 = (bf16[4,5,128,128]{3,2,1,0:T(8,128)(2,1)S(1)}, bf16[4,5,128,128]{3,2,1,0:T(8,128)(2,1)}, u32[]{:S(2)}, u32[]{:S(2)}) collective-permute-start(bf16[4,5,128,128]{3,2,1,0:T(8,128)(2,1)S(1)} %all_to_all.26), channel_id=1, source_target_pairs={{8,0},{0,1},{13,2},{6,3},{5,4},{10,5},{3,6},{15,7},{12,8},{4,9},{9... | collective-permute-start | bytes 1966088 | tf_op jit(solution)/shard_map/ppermute | solution.py:273
  82.1 12.3 %all-to-all-start.1 = ((bf16[4,5,128,128]{3,2,1,0:T(8,128)(2,1)}), bf16[4,5,128,128]{3,2,1,0:T(8,128)(2,1)S(1)}, u32[]{:S(2)}, u32[]{:S(2)}) async-start(bf16[4,5,128,128]{3,2,1,0:T(8,128)(2,1)} %get-tuple-element.13), calls=%async_computation.1 | async-start | bytes 1310720 | tf_op jit(solution)/shard_map/all_to_all | solution.py:265
  85.6 29.8 %collective-permute-start.8 = (bf16[4,5,128,128]{3,2,1,0:T(8,128)(2,1)S(1)}, bf16[4,5,128,128]{3,2,1,0:T(8,128)(2,1)}, u32[]{:S(2)}, u32[]{:S(2)}) collective-permute-start(bf16[4,5,128,128]{3,2,1,0:T(8,128)(2,1)S(1)} %all_to_all.27), channel_id=1, source_target_pairs={{3,0},{14,1},{9,2},{11,3},{8,4},{6,5},{5,6},{0,7},{7,8},{2,9},{13,... | collective-permute-start | bytes 1966088 | tf_op jit(solution)/shard_map/ppermute | solution.py:273
  89.1 33.7 %collective-permute-start = (bf16[4,5,128,128]{3,2,1,0:T(8,128)(2,1)S(1)}, bf16[4,5,128,128]{3,2,1,0:T(8,128)(2,1)}, u32[]{:S(2)}, u32[]{:S(2)}) collective-permute-start(bf16[4,5,128,128]{3,2,1,0:T(8,128)(2,1)S(1)} %all-to-all-done), channel_id=1, source_target_pairs={{4,0},{1,1},{14,2},{3,3},{11,4},{2,5},{13,6},{8,7},{0,8},{5,9},{10... | collective-permute-start | bytes 1966088 | tf_op jit(solution)/shard_map/ppermute | solution.py:273
  94.4 51.2 %collective-permute-start.2 = (bf16[4,5,128,128]{3,2,1,0:T(8,128)(2,1)S(1)}, bf16[4,5,128,128]{3,2,1,0:T(8,128)(2,1)S(1)}, u32[]{:S(2)}, u32[]{:S(2)}) collective-permute-start(bf16[4,5,128,128]{3,2,1,0:T(8,128)(2,1)S(1)} %all-to-all-done.1), channel_id=1, source_target_pairs={{12,0},{6,1},{1,2},{0,3},{3,4},{14,5},{10,6},{11,7},{8,8},{13,9},{... | collective-permute-start | bytes 1966088 | tf_op jit(solution)/shard_map/ppermute | solution.py:273
  96.9 49.6 %collective-permute-start.9 = (bf16[2,2,5,128,128]{4,3,2,1,0:T(8,128)(2,1)}, bf16[2,2,5,128,128]{4,3,2,1,0:T(8,128)(2,1)S(1)}, u32[]{:S(2)}, u32[]{:S(2)}) collective-permute-start(bf16[2,2,5,128,128]{4,3,2,1,0:T(8,128)(2,1)} %bitcast.11.refs_4_), channel_id=1, source_target_pairs={{0,1},{1,0},{2,3},{3,2},{4,5},{5,4},{6,7},{7,6},{8,9},{9,8},{10,11... | collective-permute-start | bytes 1966088 | tf_op jit(solution)/shard_map/ppermute | solution.py:236
  102.9 68.5 %collective-permute-start.12 = (bf16[2,2,5,128,128]{4,3,2,1,0:T(8,128)(2,1)}, bf16[2,2,5,128,128]{4,3,2,1,0:T(8,128)(2,1)}, u32[]{:S(2)}, u32[]{:S(2)}) collective-permute-start(bf16[2,2,5,128,128]{4,3,2,1,0:T(8,128)(2,1)} %bitcast.11.refs_4_), channel_id=1, source_target_pairs={{0,16},{1,17},{2,18},{3,19},{4,20},{5,21},{6,22},{7,23},{8,24},{9,... | collective-permute-start | bytes 1966088 | tf_op jit(solution)/shard_map/ppermute | solution.py:236
  115.4 56.0 %collective-permute-start.11 = (bf16[2,2,5,128,128]{4,3,2,1,0:T(8,128)(2,1)}, bf16[2,2,5,128,128]{4,3,2,1,0:T(8,128)(2,1)}, u32[]{:S(2)}, u32[]{:S(2)}) collective-permute-start(bf16[2,2,5,128,128]{4,3,2,1,0:T(8,128)(2,1)} %bitcast.13.refs_6_), channel_id=1, source_target_pairs={{0,1},{1,0},{2,3},{3,2},{4,5},{5,4},{6,7},{7,6},{8,9},{9,8},{10,11... | collective-permute-start | bytes 1966088 | tf_op jit(solution)/shard_map/ppermute | solution.py:236
  122.8 62.2 %collective-permute-start.14 = (bf16[2,2,5,128,128]{4,3,2,1,0:T(8,128)(2,1)}, bf16[2,2,5,128,128]{4,3,2,1,0:T(8,128)(2,1)S(1)}, u32[]{:S(2)}, u32[]{:S(2)}) collective-permute-start(bf16[2,2,5,128,128]{4,3,2,1,0:T(8,128)(2,1)} %bitcast.13.refs_6_), channel_id=1, source_target_pairs={{0,16},{1,17},{2,18},{3,19},{4,20},{5,21},{6,22},{7,23},{8,24},{9,... | collective-permute-start | bytes 1966088 | tf_op jit(solution)/shard_map/ppermute | solution.py:236
  145.6 0.9 copy-start.2
  145.6 41.5 %collective-permute-start.15 = (bf16[2,2,5,128,128]{4,3,2,1,0:T(8,128)(2,1)}, bf16[2,2,5,128,128]{4,3,2,1,0:T(8,128)(2,1)S(1)}, u32[]{:S(2)}, u32[]{:S(2)}) collective-permute-start(bf16[2,2,5,128,128]{4,3,2,1,0:T(8,128)(2,1)} %bitcast.5.refs_7_), channel_id=1, source_target_pairs={{0,16},{1,17},{2,18},{3,19},{4,20},{5,21},{6,22},{7,23},{8,24},{9,... | collective-permute-start | bytes 1966088 | tf_op jit(solution)/shard_map/ppermute | solution.py:236
  146.5 69.3 %copy-start.3 = (bf16[2,2,5,128,128]{4,3,2,1,0:T(8,128)(2,1)}, bf16[2,2,5,128,128]{4,3,2,1,0:T(8,128)(2,1)S(1)}, u32[]{:S(2)}) copy-start(bf16[2,2,5,128,128]{4,3,2,1,0:T(8,128)(2,1)S(1)} %collective-permute-done.9.refs_9_) | copy-start | bytes 1966084
  146.5 38.2 %collective-permute-start.7 = (bf16[4,5,128,128]{3,2,1,0:T(8,128)(2,1)S(1)}, bf16[4,5,128,128]{3,2,1,0:T(8,128)(2,1)}, u32[]{:S(2)}, u32[]{:S(2)}) collective-permute-start(bf16[4,5,128,128]{3,2,1,0:T(8,128)(2,1)S(1)} %all_to_all.25), channel_id=1, source_target_pairs={{11,0},{9,1},{5,2},{8,3},{0,4},{13,5},{2,6},{7,7},{15,8},{10,9},{1... | collective-permute-start | bytes 1966088 | tf_op jit(solution)/shard_map/ppermute | solution.py:273
  171.4 17.6 %collective-permute-start.1 = (bf16[2,2,5,128,128]{4,3,2,1,0:T(8,128)(2,1)}, bf16[2,2,5,128,128]{4,3,2,1,0:T(8,128)(2,1)S(1)}, u32[]{:S(2)}, u32[]{:S(2)}) collective-permute-start(bf16[2,2,5,128,128]{4,3,2,1,0:T(8,128)(2,1)} %bitcast.5.refs_7_), channel_id=1, source_target_pairs={{0,1},{1,0},{2,3},{3,2},{4,5},{5,4},{6,7},{7,6},{8,9},{9,8},{10,11... | collective-permute-start | bytes 1966088 | tf_op jit(solution)/shard_map/ppermute | solution.py:236
  171.4 15.7 %collective-permute-start.16 = (bf16[2,2,5,128,128]{4,3,2,1,0:T(8,128)(2,1)}, bf16[2,2,5,128,128]{4,3,2,1,0:T(8,128)(2,1)}, u32[]{:S(2)}, u32[]{:S(2)}) collective-permute-start(bf16[2,2,5,128,128]{4,3,2,1,0:T(8,128)(2,1)} %bitcast.19), channel_id=1, source_target_pairs={{0,16},{1,17},{2,18},{3,19},{4,20},{5,21},{6,22},{7,23},{8,24},{9,... | collective-permute-start | bytes 1966088 | tf_op jit(solution)/shard_map/ppermute | solution.py:236
  184.7 18.5 %collective-permute-start.10 = (bf16[2,2,5,128,128]{4,3,2,1,0:T(8,128)(2,1)}, bf16[2,2,5,128,128]{4,3,2,1,0:T(8,128)(2,1)}, u32[]{:S(2)}, u32[]{:S(2)}) collective-permute-start(bf16[2,2,5,128,128]{4,3,2,1,0:T(8,128)(2,1)} %bitcast.12.refs_5_), channel_id=1, source_target_pairs={{0,1},{1,0},{2,3},{3,2},{4,5},{5,4},{6,7},{7,6},{8,9},{9,8},{10,11... | collective-permute-start | bytes 1966088 | tf_op jit(solution)/shard_map/ppermute | solution.py:236
  185.0 18.7 %copy-start.4 = (bf16[2,2,5,128,128]{4,3,2,1,0:T(8,128)(2,1)}, bf16[2,2,5,128,128]{4,3,2,1,0:T(8,128)(2,1)S(1)}, u32[]{:S(2)}) copy-start(bf16[2,2,5,128,128]{4,3,2,1,0:T(8,128)(2,1)S(1)} %collective-permute-done.14.refs_14_) | copy-start | bytes 1966084
  185.0 30.8 %collective-permute-start.3 = (bf16[2,2,5,128,128]{4,3,2,1,0:T(8,128)(2,1)}, bf16[2,2,5,128,128]{4,3,2,1,0:T(8,128)(2,1)S(1)}, u32[]{:S(2)}, u32[]{:S(2)}) collective-permute-start(bf16[2,2,5,128,128]{4,3,2,1,0:T(8,128)(2,1)} %bitcast.20), channel_id=1, source_target_pairs={{0,1},{1,0},{2,3},{3,2},{4,5},{5,4},{6,7},{7,6},{8,9},{9,8},{10,11... | collective-permute-start | bytes 1966088 | tf_op jit(solution)/shard_map/ppermute | solution.py:236
  187.1 31.9 %copy-start.5 = (bf16[2,2,5,128,128]{4,3,2,1,0:T(8,128)(2,1)}, bf16[2,2,5,128,128]{4,3,2,1,0:T(8,128)(2,1)S(1)}, u32[]{:S(2)}) copy-start(bf16[2,2,5,128,128]{4,3,2,1,0:T(8,128)(2,1)S(1)} %collective-permute-done.15.refs_15_) | copy-start | bytes 1966084
  187.1 28.7 %collective-permute-start.17 = (bf16[2,2,5,128,128]{4,3,2,1,0:T(8,128)(2,1)S(1)}, bf16[2,2,5,128,128]{4,3,2,1,0:T(8,128)(2,1)S(1)}, u32[]{:S(2)}, u32[]{:S(2)}) collective-permute-start(bf16[2,2,5,128,128]{4,3,2,1,0:T(8,128)(2,1)S(1)} %collective-permute-done.9.refs_9_), channel_id=1, source_target_pairs={{0,16},{1,17},{2,18},{3,19},{4,20},{5,21},{6,22},{7,23},{8,24},{9,... | collective-permute-start | bytes 1966088 | tf_op jit(solution)/shard_map/ppermute | solution.py:236
  187.1 31.9 %collective-permute-start.19 = (bf16[2,2,5,128,128]{4,3,2,1,0:T(8,128)(2,1)}, bf16[2,2,5,128,128]{4,3,2,1,0:T(8,128)(2,1)}, u32[]{:S(2)}, u32[]{:S(2)}) collective-permute-start(bf16[2,2,5,128,128]{4,3,2,1,0:T(8,128)(2,1)} %collective-permute-done.11.refs_11_), channel_id=1, source_target_pairs={{0,16},{1,17},{2,18},{3,19},{4,20},{5,21},{6,22},{7,23},{8,24},{9,... | collective-permute-start | bytes 1966088 | tf_op jit(solution)/shard_map/ppermute | solution.py:236
  189.0 29.9 %collective-permute-start.13 = (bf16[2,2,5,128,128]{4,3,2,1,0:T(8,128)(2,1)}, bf16[2,2,5,128,128]{4,3,2,1,0:T(8,128)(2,1)}, u32[]{:S(2)}, u32[]{:S(2)}) collective-permute-start(bf16[2,2,5,128,128]{4,3,2,1,0:T(8,128)(2,1)} %bitcast.12.refs_5_), channel_id=1, source_target_pairs={{0,16},{1,17},{2,18},{3,19},{4,20},{5,21},{6,22},{7,23},{8,24},{9,... | collective-permute-start | bytes 1966088 | tf_op jit(solution)/shard_map/ppermute | solution.py:236
  203.2 15.8 %collective-permute-start.18 = (bf16[2,2,5,128,128]{4,3,2,1,0:T(8,128)(2,1)}, bf16[2,2,5,128,128]{4,3,2,1,0:T(8,128)(2,1)}, u32[]{:S(2)}, u32[]{:S(2)}) collective-permute-start(bf16[2,2,5,128,128]{4,3,2,1,0:T(8,128)(2,1)} %collective-permute-done.10.refs_10_), channel_id=1, source_target_pairs={{0,16},{1,17},{2,18},{3,19},{4,20},{5,21},{6,22},{7,23},{8,24},{9,... | collective-permute-start | bytes 1966088 | tf_op jit(solution)/shard_map/ppermute | solution.py:236
  215.7 20.8 %collective-permute-start.4 = (bf16[2,2,5,128,128]{4,3,2,1,0:T(8,128)(2,1)S(1)}, bf16[2,2,5,128,128]{4,3,2,1,0:T(8,128)(2,1)S(1)}, u32[]{:S(2)}, u32[]{:S(2)}) collective-permute-start(bf16[2,2,5,128,128]{4,3,2,1,0:T(8,128)(2,1)S(1)} %collective-permute-done.1.refs_0_), channel_id=1, source_target_pairs={{0,16},{1,17},{2,18},{3,19},{4,20},{5,21},{6,22},{7,23},{8,24},{9,... | collective-permute-start | bytes 1966088 | tf_op jit(solution)/shard_map/ppermute | solution.py:236
  215.8 0.9 copy-start.6
  216.6 19.9 %collective-permute-start.5 = (bf16[2,2,5,128,128]{4,3,2,1,0:T(8,128)(2,1)S(1)}, bf16[2,2,5,128,128]{4,3,2,1,0:T(8,128)(2,1)S(1)}, u32[]{:S(2)}, u32[]{:S(2)}) collective-permute-start(bf16[2,2,5,128,128]{4,3,2,1,0:T(8,128)(2,1)S(1)} %collective-permute-done.3.refs_1_), channel_id=1, source_target_pairs={{0,16},{1,17},{2,18},{3,19},{4,20},{5,21},{6,22},{7,23},{8,24},{9,... | collective-permute-start | bytes 1966088 | tf_op jit(solution)/shard_map/ppermute | solution.py:236
  219.0 17.5 %copy-start.1 = (s32[71]{0:T(128)S(1)}, s32[71]{0:T(128)}, u32[]{:S(2)}) copy-start(s32[71]{0:T(128)} %concatenate.8.refs_0_.scal) | copy-start | bytes 856
Sparse Core Ops, SparseCore 0:
  9.0 25.4 all-gather.3
  36.1 33.4 all-gather.7
  71.3 85.0 all-gather.5

commit v2 on v1

--- a/solution.py
+++ b/solution.py
@@ -94,7 +94,7 @@
     )(where, children.reshape(KR, XS, TILE, KC * TILE))
 
 
-CORE, SLOT, COL_ON, ROW_ON = 0, 1, 11, 31
+CORE, SLOT, COL_ON, ROW_ON, PIECE, IS_HERE = 0, 1, 11, 31, 71, 87
 UNIT = (2, 1, KR, TILE, TILE)
 HEIGHT = KR * TILE
 
@@ -124,13 +124,29 @@
                     out[rows, pl.ds(start, TILE)] += unit[child, 0, kk].astype(jnp.float32)
 
 
-def base_kernel(spots, scal, listed, lower, upper, *refs):
-    units, out = refs[:-1], refs[-1]
+def base_kernel(spots, scal, listed, *refs):
+    lower, refs = refs[:8], refs[8:]
+    up_here, up_core, units, out, upper = refs[0], refs[1], refs[2:-2], refs[-2], refs[-1]
     block = pl.program_id(0)
     same = block % 2 == scal[CORE]
+
+    @pl.when(block == 0)
+    def _():
+        for i in range(COLS):
+            at, here = scal[PIECE + i], scal[IS_HERE + i]
+
+            @pl.when(here == 1)
+            def _():
+                upper[pl.ds(i * 64, 64), :] = up_here[at]
+
+            @pl.when(here == 0)
+            def _():
+                upper[pl.ds(i * 64, 64), :] = up_core[at]
+
     for kk in range(KR):
         rows = pl.ds(kk * TILE, TILE)
-        acc = jnp.dot(lower[rows, :], upper[...], preferred_element_type=jnp.float32)
+        left = jnp.concatenate([piece[rows, :] for piece in lower], axis=1)
+        acc = jnp.dot(left, upper[...], preferred_element_type=jnp.float32)
         out[rows, :] = jnp.where(listed[block * KR + kk] > 0.5, -acc, 0.0)
 
     def add(group):
@@ -147,19 +163,19 @@
         add(units[len(spots) :])
 
 
-def base(scal, listed, lower, upper, spots, own, other):
+def base(scal, listed, lower, up_here, up_core, spots, own, other):
     n = len(spots)
+    whole = pl.BlockSpec((8, 64, PC * TILE), lambda b, s: (0, 0, 0), pipeline_mode=pl.Buffered(1))
     spec = pltpu.PrefetchScalarGridSpec(
         num_scalar_prefetch=1,
         grid=(PRB // KR,),
-        in_specs=[
-            pl.BlockSpec((PRB, 1, PC * TILE), lambda b, s: (0, 0, 0)),
-            pl.BlockSpec((HEIGHT, 1024), lambda b, s: (b, 0)),
-            pl.BlockSpec((1024, PC * TILE), lambda b, s: (0, 0)),
-        ]
+        in_specs=[pl.BlockSpec((PRB, 1, PC * TILE), lambda b, s: (0, 0, 0))]
+        + [pl.BlockSpec((HEIGHT, TILE), lambda b, s: (b, 0))] * 8
+        + [whole, whole]
         + [pl.BlockSpec(UNIT, own_map)] * n
         + [pl.BlockSpec(UNIT, other_map)] * n,
         out_specs=pl.BlockSpec((HEIGHT, PC * TILE), lambda b, s: (b, 0)),
+        scratch_shapes=[pltpu.VMEM((1024, PC * TILE), jnp.bfloat16)],
     )
 
     def kernel(*refs):
@@ -174,57 +190,23 @@
             flops=2 * 2560 * 1280 * 1024, bytes_accessed=34 << 20, transcendentals=0
         ),
         name="base",
-    )(scal, listed, lower, upper, *own, *other)
-
-
-def tail(scal, front, spots, own, other):
-    n = len(spots)
-
-    def kernel(scal, *refs):
-        units, fronts, out = refs[: 2 * n], refs[2 * n], refs[2 * n + 1]
-        block = pl.program_id(1)
-        same = block % 2 == scal[CORE]
-        out[...] = fronts[...]
-        for i, spot in enumerate(spots):
-
-            @pl.when((pl.program_id(0) == i) & same)
-            def _():
-                add_unit(scal, spot, block, units[i], out, 0)
-
-            @pl.when((pl.program_id(0) == i) & jnp.logical_not(same))
-            def _():
-                add_unit(scal, spot, block, units[n + i], out, 0)
-
-    def front_map(i, b, s):
-        slot = s[SLOT + spots[0]]
-        for j in range(1, n):
-            slot = jnp.where(i == j, s[SLOT + spots[j]], slot)
-        return (b, slot)
-
-    def unit_map(index, pick):
-        def at(i, b, s):
-            now = jnp.where(i == index, b, jnp.where(i < index, 0, PRB // KR - 1))
-            return pick(now, s)
-
-        return at
-
-    spec = pltpu.PrefetchScalarGridSpec(
-        num_scalar_prefetch=1,
-        grid=(n, PRB // KR),
-        in_specs=[pl.BlockSpec(UNIT, unit_map(i, own_map)) for i in range(n)]
-        + [pl.BlockSpec(UNIT, unit_map(i, other_map)) for i in range(n)]
-        + [pl.BlockSpec((HEIGHT, TILE), front_map)],
-        out_specs=pl.BlockSpec((HEIGHT, TILE), front_map),
-    )
+    )(scal, listed, *lower, up_here, up_core, *own, *other)
+
+
+def turn_kernel(a, b, out):
+    out[...] = jnp.concatenate([a[...], b[...]], axis=0).T
+
+
+def turn(a, b):
     return pl.pallas_call(
-        kernel,
-        grid_spec=spec,
-        out_shape=jax.ShapeDtypeStruct((PRB * TILE, PC * TILE), jnp.float32),
-        input_output_aliases={2 * n + 1: 0},
-        compiler_params=pltpu.CompilerParams(vmem_limit_bytes=32 << 20),
-        cost_estimate=pl.CostEstimate(flops=0, bytes_accessed=8 << 20, transcendentals=0),
-        name="tail",
-    )(scal, *own, *other, front)
+        turn_kernel,
+        grid=(2,),
+        in_specs=[pl.BlockSpec((64, 1280), lambda i: (0, i))] * 2,
+        out_specs=pl.BlockSpec((1280, TILE), lambda i: (i, 0)),
+        out_shape=jax.ShapeDtypeStruct((PRB * TILE, TILE), jnp.bfloat16),
+        cost_estimate=pl.CostEstimate(flops=0, bytes_accessed=1310720, transcendentals=0),
+        name="turn",
+    )(a, b)
 
 
 def hop(array, row_mask=0, col_mask=0):
@@ -250,32 +232,46 @@
             tile_of[r, j // KC] = j % KC
             slot_of[r, target] = j // 8
 
-    along_z = [[4 * y + z for z in range(4)] for y in range(4)]
-    along_y = [[4 * y + z for y in range(4)] for z in range(4)]
-    lower_here = lax.all_gather(
-        lower_panel.T, "col", axis=0, tiled=True, axis_index_groups=along_z
-    )
-    upper_all = lax.all_gather(upper_panel, "row", axis=0, tiled=True)
+    low = lower_panel.T
+    low_a = turn(low, hop(low, col_mask=1))
+    low_b = hop(low_a, col_mask=3)
+    low_1a = hop(low_a, col_mask=4)
+    low_3a = hop(low_a, col_mask=12)
+    low_1b = hop(low_b, col_mask=4)
+    low_3b = hop(low_b, col_mask=12)
+    low_2a = hop(low_1a, col_mask=12)
+    low_2b = hop(low_3b, col_mask=4)
+    lower = [low_a, low_b, low_1a, low_1b, low_3a, low_3b, low_2a, low_2b]
+    shard = col ^ jnp.asarray(
+        [4 * y + z for y in (0, 1, 3, 2) for z in (0, 1, 3, 2)], jnp.int32
+    )
+
+    up01 = jnp.concatenate([upper_panel, hop(upper_panel, row_mask=2)])
+    up_here = jnp.concatenate([up01, hop(up01, row_mask=6)])
+    up_core = hop(up_here, row_mask=1)
+    away = row ^ (shard >> 1)
+    far = away >> 1
+    place = jnp.where(far >= 2, 5 - far, far)
+    piece = place * 2 + (shard & 1)
+    is_here = 1 - (away & 1)
 
     packed = pack(children, jnp.asarray(tile_of)[:, col])
 
-    held, swapped, core_held, core_swapped = [], [], [], []
-    same_core = [[2 * x + c for x in range(XS)] for c in range(2)]
-    for r in range(ROUNDS):
-        got = lax.all_to_all(
-            packed[r], "row", 0, 0, axis_index_groups=same_core, tiled=True
-        )
-        if r == 1:
-            lower_here, got = lax.optimization_barrier((lower_here, got))
-            lower_all = lax.all_gather(
-                lower_here, "col", axis=0, tiled=True, axis_index_groups=along_y
-            ).T
-        got = lax.ppermute(got, "col", [(source_of[r][q], q) for q in range(COLS)])
-        held.append(got.reshape(UNIT[0], 2, KR, TILE, TILE))
-    for r in range(ROUNDS):
+    def to_chip(array):
+        groups = [[2 * x + c for x in range(XS)] for c in range(2)]
+        return lax.all_to_all(array, "row", 0, 0, axis_index_groups=groups, tiled=True)
+
+    def to_holder(array, r):
+        return lax.ppermute(array, "col", [(source_of[r][q], q) for q in range(COLS)])
+
+    first = to_holder(packed[0], 0)
+    held = [to_chip(first)]
+    swapped = [to_chip(hop(first, col_mask=1))]
+    for r in range(1, ROUNDS):
+        held.append(to_holder(to_chip(packed[r]), r))
         swapped.append(hop(held[r], col_mask=1))
-        core_held.append(hop(held[r], row_mask=1))
-        core_swapped.append(hop(swapped[r], row_mask=1))
+    core_held = [hop(array, row_mask=1) for array in held]
+    core_swapped = [hop(array, row_mask=1) for array in swapped]
 
     slots = jnp.arange(PRB, dtype=jnp.int32)
     row_on = lax.dynamic_slice_in_dim(row_maps.reshape(2, PRB, XS), chip, 1, 2)[:, :, 0]
@@ -293,6 +289,8 @@
             slot,
             by_slot.reshape(-1),
             row_on.reshape(-1),
+            piece,
+            is_here,
         ]
     ).astype(jnp.int32)
 
@@ -301,20 +299,19 @@
     listed = jnp.dot(row_hit.T, col_hit, preferred_element_type=jnp.float32)
     listed = jnp.repeat(listed, TILE, axis=1).reshape(PRB, 1, PC * TILE)
 
-    own = held + swapped
-    other = core_held + core_swapped
-    early = list(range(2 * ROUNDS - 2))
-    late = [2 * ROUNDS - 2, 2 * ROUNDS - 1]
-    front = base(
+    def units(arrays):
+        return [array.reshape(UNIT[0], 2, KR, TILE, TILE) for array in arrays]
+
+    return base(
         scal,
         listed,
-        lower_all,
-        upper_all,
-        early,
-        [own[i] for i in early],
-        [other[i] for i in early],
-    )
-    return tail(scal, front, late, [own[i] for i in late], [other[i] for i in late])
+        lower,
+        up_here.reshape(8, 64, PC * TILE),
+        up_core.reshape(8, 64, PC * TILE),
+        list(range(2 * ROUNDS)),
+        units(held + swapped),
+        units(core_held + core_swapped),
+    )
 
 
 def solution(mesh):

time: 255 us -> 218 us (0.85)
  the two profiles are of different devices: /device:TPU:80 before, /device:TPU:5 now
where the time goes in v2:
time: 218 us; the launch traced here: 217 us
  starting transfers between devices  127 us (58%)
  waiting for transfers between devices  46.9 us (22%)
  Pallas kernels  23.9 us (11%)
  blocking collectives  11.5 us (5%)
  local copies, waits for them, and re-layouts  5.16 us (2%)
    ppermute x26, starting transfers between devices, hop(): return lax.ppermute(array, ('row', 'col'), route)  72.7 us
    ppermute x26, waiting for transfers between devices, hop(): return lax.ppermute(array, ('row', 'col'), route)  38.6 us
    all_to_all x5, starting transfers between devices, to_chip(): lax.all_to_all(array, 'row', 0, 0, axis_index_groups=groups, tiled=True)  29 us
    ppermute x5, starting transfers between devices, to_holder(): lax.ppermute(array, 'col', [(source_of[r][q], q) for q in range(COLS)])  25.4 us
    pallas_call x1, Pallas kernels, base(): pl.pallas_call(kernel, grid_spec=spec, out_shape=jax.ShapeDtypeStruct((PR...  19.7 us
    all_to_all x1, blocking collectives, to_chip(): lax.all_to_all(array, 'row', 0, 0, axis_index_groups=groups, tiled=True)  11.5 us
    ppermute x5, waiting for transfers between devices, to_holder(): lax.ppermute(array, 'col', [(source_of[r][q], q) for q in range(COLS)])  4.62 us
  transfers between devices with their start and end apart: 36, of which 9 were waited for; matrix products, arithmetic and copies ran while one was open for 2% of the time, Pallas kernels for 1%

profile of v2, /device:TPU:5, one launch (start us, length us, event | category | flops | bytes accessed | tf_op | source)
XLA Modules:
  0.0 216.6 jit_solution(9397813263312427585)
XLA Ops:
  0.0 0.8 fusion.11
  0.8 1.9 copy-done
  2.7 2.2 %pack.1 = (bf16[4,5,128,128]{3,2,1,0:T(8,128)(2,1)S(1)}, bf16[4,5,128,128]{3,2,1,0:T(8,128)(2,1)}, bf16[4,5,128,128]{3,2,1,0:T(8,128)(2,1)S(1)}, bf16[4,5,128,12...) custom-call(s32[5]{0:T(128)S(1)} %get-tuple-element.21.where, bf16[5,4,128,640]{3,2,1,0:T(8,128)(2,1)S(1)} %bitcast.33), custom_call_target="tpu_custom_call" | custom-call | bytes 6553600 | tf_op jit(solution)/shard_map/pack/pallas_call | solution.py:87
  4.9 11.5 %all_to_all.30 = bf16[4,5,128,128]{3,2,1,0:T(8,128)(2,1)S(1)} all-to-all(bf16[4,5,128,128]{3,2,1,0:T(8,128)(2,1)S(1)} %get-tuple-element.12), channel_id=1, replica_groups={{0,32,64,96},{16,48,80,112},{1,33,65,97},{17,49,81,113},{2,34,66,98},{1..., dimensions={0} | all-to-all | bytes 1310720 | tf_op jit(solution)/shard_map/all_to_all | solution.py:262
  16.4 6.1 %all-to-all-start.3 = ((bf16[4,5,128,128]{3,2,1,0:T(8,128)(2,1)}), bf16[4,5,128,128]{3,2,1,0:T(8,128)(2,1)S(1)}, u32[]{:S(2)}, u32[]{:S(2)}) async-start(bf16[4,5,128,128]{3,2,1,0:T(8,128)(2,1)} %get-tuple-element.13), calls=%async_computation.3 | async-start | bytes 1310720 | tf_op jit(solution)/shard_map/all_to_all | solution.py:262
  22.5 0.9 collective-permute-start.8
  23.4 1.6 collective-permute-start
  25.0 3.7 %all-to-all-done.3 = bf16[4,5,128,128]{3,2,1,0:T(8,128)(2,1)S(1)} async-done(((bf16[4,5,128,128]{3,2,1,0:T(8,128)(2,1)}), bf16[4,5,128,128]{3,2,1,0:T(8,128)(2,1)S(1)}, u32[]{:S(2)}, u32[]{:S(2)}) %all-to-all-start.3) | async-done | bytes 655392 | tf_op jit(solution)/shard_map/all_to_all | solution.py:262
  28.7 6.8 %all-to-all-start.4 = ((bf16[4,5,128,128]{3,2,1,0:T(8,128)(2,1)}), bf16[4,5,128,128]{3,2,1,0:T(8,128)(2,1)}, u32[]{:S(2)}, u32[]{:S(2)}) async-start(bf16[4,5,128,128]{3,2,1,0:T(8,128)(2,1)} %get-tuple-element.14), calls=%async_computation.4 | async-start | bytes 1310720 | tf_op jit(solution)/shard_map/all_to_all | solution.py:262
  35.5 1.6 collective-permute-start.11
  37.2 0.9 pad_maximum_fusion
  38.0 0.3 collective-permute-start.9
  38.3 2.0 turn.1.refs_2_
  40.4 1.9 collective-permute-start.4
  42.3 0.4 collective-permute-start.2
  42.7 3.5 %collective-permute-start.1 = (bf16[2560,128]{1,0:T(8,128)(2,1)}, bf16[2560,128]{1,0:T(8,128)(2,1)}, u32[]{:S(2)}, u32[]{:S(2)}) collective-permute-start(bf16[2560,128]{1,0:T(8,128)(2,1)} %turn.1.refs_2_), channel_id=1, source_target_pairs={{0,3},{1,2},{2,1},{3,0},{4,7},{5,6},{6,5},{7,4},{8,11},{9,10},{10,... | collective-permute-start | bytes 1966088 | tf_op jit(solution)/shard_map/ppermute | solution.py:218
  46.2 6.5 %all-to-all-start.1 = ((bf16[4,5,128,128]{3,2,1,0:T(8,128)(2,1)}), bf16[4,5,128,128]{3,2,1,0:T(8,128)(2,1)}, u32[]{:S(2)}, u32[]{:S(2)}) async-start(bf16[4,5,128,128]{3,2,1,0:T(8,128)(2,1)} %get-tuple-element.11), calls=%async_computation.1 | async-start | bytes 1310720 | tf_op jit(solution)/shard_map/all_to_all | solution.py:262
  52.7 1.9 collective-permute-start.15
  54.6 1.4 collective-permute-done.9
  56.0 6.6 %collective-permute-start.14 = (bf16[4,5,128,128]{3,2,1,0:T(8,128)(2,1)S(1)}, bf16[4,5,128,128]{3,2,1,0:T(8,128)(2,1)S(1)}, u32[]{:S(2)}, u32[]{:S(2)}) collective-permute-start(bf16[4,5,128,128]{3,2,1,0:T(8,128)(2,1)S(1)} %all-to-all-done.3), channel_id=1, source_target_pairs={{4,0},{1,1},{14,2},{3,3},{11,4},{2,5},{13,6},{8,7},{0,8},{5,9},{10... | collective-permute-start | bytes 1966088 | tf_op jit(solution)/shard_map/ppermute | solution.py:265
  62.6 3.7 %collective-permute-done.4.refs_6_ = bf16[2560,128]{1,0:T(8,128)(2,1)} collective-permute-done((bf16[2560,128]{1,0:T(8,128)(2,1)}, bf16[2560,128]{1,0:T(8,128)(2,1)}, u32[]{:S(2)}, u32[]{:S(2)}) %collective-permute-start.4) | collective-permute-done | bytes 655392 | tf_op jit(solution)/shard_map/ppermute | solution.py:218
  66.3 7.2 %collective-permute-start.13 = (bf16[4,5,128,128]{3,2,1,0:T(8,128)(2,1)S(1)}, bf16[4,5,128,128]{3,2,1,0:T(8,128)(2,1)}, u32[]{:S(2)}, u32[]{:S(2)}) collective-permute-start(bf16[4,5,128,128]{3,2,1,0:T(8,128)(2,1)S(1)} %all_to_all.30), channel_id=1, source_target_pairs={{3,0},{14,1},{9,2},{11,3},{8,4},{6,5},{5,6},{0,7},{7,8},{2,9},{13,... | collective-permute-start | bytes 1966088 | tf_op jit(solution)/shard_map/ppermute | solution.py:265
  73.5 8.1 %collective-permute-start.12 = (bf16[4,5,128,128]{3,2,1,0:T(8,128)(2,1)}, bf16[4,5,128,128]{3,2,1,0:T(8,128)(2,1)S(1)}, u32[]{:S(2)}, u32[]{:S(2)}) collective-permute-start(bf16[4,5,128,128]{3,2,1,0:T(8,128)(2,1)} %all-to-all-done.1), channel_id=1, source_target_pairs={{11,0},{9,1},{5,2},{8,3},{0,4},{13,5},{2,6},{7,7},{15,8},{10,9},{1... | collective-permute-start | bytes 1966088 | tf_op jit(solution)/shard_map/ppermute | solution.py:265
  81.6 0.1 collective-permute-start.16
  81.7 4.5 %collective-permute-start.5 = (bf16[2560,128]{1,0:T(8,128)(2,1)}, bf16[2560,128]{1,0:T(8,128)(2,1)}, u32[]{:S(2)}, u32[]{:S(2)}) collective-permute-start(bf16[2560,128]{1,0:T(8,128)(2,1)} %collective-permute-done.1.refs_3_), channel_id=1, source_target_pairs={{0,12},{1,13},{2,14},{3,15},{4,8},{5,9},{6,10},{7,11},{8,4},{9,5},... | collective-permute-start | bytes 1966088 | tf_op jit(solution)/shard_map/ppermute | solution.py:218
  86.2 13.3 %collective-permute-start.3 = (bf16[2560,128]{1,0:T(8,128)(2,1)}, bf16[2560,128]{1,0:T(8,128)(2,1)}, u32[]{:S(2)}, u32[]{:S(2)}) collective-permute-start(bf16[2560,128]{1,0:T(8,128)(2,1)} %collective-permute-done.1.refs_3_), channel_id=1, source_target_pairs={{0,4},{1,5},{2,6},{3,7},{4,0},{5,1},{6,2},{7,3},{8,12},{9,13},{10,... | collective-permute-start | bytes 1966088 | tf_op jit(solution)/shard_map/ppermute | solution.py:218
  99.6 4.6 %collective-permute-done.12 = bf16[4,5,128,128]{3,2,1,0:T(8,128)(2,1)S(1)} collective-permute-done((bf16[4,5,128,128]{3,2,1,0:T(8,128)(2,1)}, bf16[4,5,128,128]{3,2,1,0:T(8,128)(2,1)S(1)}, u32[]{:S(2)}, u32[]{:S(2)}) %collective-permute-start.12) | collective-permute-done | bytes 655392 | tf_op jit(solution)/shard_map/ppermute | solution.py:265
  104.2 8.7 %collective-permute-start.25 = (bf16[4,5,128,128]{3,2,1,0:T(8,128)(2,1)}, bf16[4,5,128,128]{3,2,1,0:T(8,128)(2,1)}, u32[]{:S(2)}, u32[]{:S(2)}) collective-permute-start(bf16[4,5,128,128]{3,2,1,0:T(8,128)(2,1)} %collective-permute-done.15), channel_id=1, source_target_pairs={{0,16},{1,17},{2,18},{3,19},{4,20},{5,21},{6,22},{7,23},{8,24},{9,... | collective-permute-start | bytes 1966088 | tf_op jit(solution)/shard_map/ppermute | solution.py:218
  112.9 15.4 %collective-permute-start.20 = (bf16[4,5,128,128]{3,2,1,0:T(8,128)(2,1)}, bf16[4,5,128,128]{3,2,1,0:T(8,128)(2,1)}, u32[]{:S(2)}, u32[]{:S(2)}) collective-permute-start(bf16[4,5,128,128]{3,2,1,0:T(8,128)(2,1)} %collective-permute-done.15), channel_id=1, source_target_pairs={{0,1},{1,0},{2,3},{3,2},{4,5},{5,4},{6,7},{7,6},{8,9},{9,8},{10,11... | collective-permute-start | bytes 1966088 | tf_op jit(solution)/shard_map/ppermute | solution.py:218
  128.3 5.2 %all-to-all-start = ((bf16[4,5,128,128]{3,2,1,0:T(8,128)(2,1)}), bf16[4,5,128,128]{3,2,1,0:T(8,128)(2,1)S(1)}, u32[]{:S(2)}, u32[]{:S(2)}) async-start(bf16[4,5,128,128]{3,2,1,0:T(8,128)(2,1)} %collective-permute-done.11), calls=%async_computation | async-start | bytes 1310720 | tf_op jit(solution)/shard_map/all_to_all | solution.py:262
  133.6 2.4 %collective-permute-done.6.refs_8_ = bf16[2560,128]{1,0:T(8,128)(2,1)} collective-permute-done((bf16[2560,128]{1,0:T(8,128)(2,1)}, bf16[2560,128]{1,0:T(8,128)(2,1)}, u32[]{:S(2)}, u32[]{:S(2)}) %collective-permute-start.6) | collective-permute-done | bytes 655392 | tf_op jit(solution)/shard_map/ppermute | solution.py:218
  136.0 0.5 collective-permute-start.10
  136.5 0.1 collective-permute-start.24
  136.6 11.0 %collective-permute-start.19 = (bf16[4,5,128,128]{3,2,1,0:T(8,128)(2,1)S(1)}, bf16[4,5,128,128]{3,2,1,0:T(8,128)(2,1)}, u32[]{:S(2)}, u32[]{:S(2)}) collective-permute-start(bf16[4,5,128,128]{3,2,1,0:T(8,128)(2,1)S(1)} %copy-done.6), channel_id=1, source_target_pairs={{0,1},{1,0},{2,3},{3,2},{4,5},{5,4},{6,7},{7,6},{8,9},{9,8},{10,11... | collective-permute-start | bytes 1966088 | tf_op jit(solution)/shard_map/ppermute | solution.py:218
  147.6 0.7 collective-permute-start.23
  148.3 0.1 fusion.14
  148.4 0.1 reshape.131
  148.5 0.2 dynamic-slice_reduce_fusion.1
  148.7 0.3 collective-permute-start.22
  149.0 13.5 %collective-permute-done.19 = bf16[4,5,128,128]{3,2,1,0:T(8,128)(2,1)} collective-permute-done((bf16[4,5,128,128]{3,2,1,0:T(8,128)(2,1)S(1)}, bf16[4,5,128,128]{3,2,1,0:T(8,128)(2,1)}, u32[]{:S(2)}, u32[]{:S(2)}) %collective-permute-start.19) | collective-permute-done | bytes 655392 | tf_op jit(solution)/shard_map/ppermute | solution.py:218
  162.4 1.2 collective-permute-start.17
  163.6 2.5 %collective-permute-start.21 = (bf16[4,5,128,128]{3,2,1,0:T(8,128)(2,1)S(1)}, bf16[4,5,128,128]{3,2,1,0:T(8,128)(2,1)}, u32[]{:S(2)}, u32[]{:S(2)}) collective-permute-start(bf16[4,5,128,128]{3,2,1,0:T(8,128)(2,1)S(1)} %all-to-all-done), channel_id=1, source_target_pairs={{0,16},{1,17},{2,18},{3,19},{4,20},{5,21},{6,22},{7,23},{8,24},{9,... | collective-permute-start | bytes 1966088 | tf_op jit(solution)/shard_map/ppermute | solution.py:218
  166.1 10.3 %collective-permute-done.18 = bf16[4,5,128,128]{3,2,1,0:T(8,128)(2,1)} collective-permute-done((bf16[4,5,128,128]{3,2,1,0:T(8,128)(2,1)}, bf16[4,5,128,128]{3,2,1,0:T(8,128)(2,1)}, u32[]{:S(2)}, u32[]{:S(2)}) %collective-permute-start.18) | collective-permute-done | bytes 655392 | tf_op jit(solution)/shard_map/ppermute | solution.py:218
  176.5 4.2 %all-to-all-start.5 = ((bf16[4,5,128,128]{3,2,1,0:T(8,128)(2,1)}), bf16[4,5,128,128]{3,2,1,0:T(8,128)(2,1)S(1)}, u32[]{:S(2)}, u32[]{:S(2)}) async-start(bf16[4,5,128,128]{3,2,1,0:T(8,128)(2,1)} %collective-permute-done.16), calls=%async_computation.5 | async-start | bytes 1310720 | tf_op jit(solution)/shard_map/all_to_all | solution.py:262
  180.8 0.1 eq.76
  180.8 0.1 pad_add_fusion
  180.9 0.1 fusion.7
  181.0 0.2 multiply_reduce_fusion
  181.2 0.1 reshape.132
  181.3 0.1 reshape.133
  181.4 0.2 dynamic-slice_reduce_fusion
  181.6 0.1 squeeze.18
  181.7 2.2 collective-permute-start.30
  183.9 6.7 %collective-permute-done.17 = bf16[4,5,128,128]{3,2,1,0:T(8,128)(2,1)S(1)} collective-permute-done((bf16[4,5,128,128]{3,2,1,0:T(8,128)(2,1)}, bf16[4,5,128,128]{3,2,1,0:T(8,128)(2,1)S(1)}, u32[]{:S(2)}, u32[]{:S(2)}) %collective-permute-start.17) | collective-permute-done | bytes 655392 | tf_op jit(solution)/shard_map/ppermute | solution.py:218
  190.5 0.9 collective-permute-start.29
  191.4 0.1 collective-permute-start.28
  191.5 2.4 %collective-permute-start.27 = (bf16[4,5,128,128]{3,2,1,0:T(8,128)(2,1)S(1)}, bf16[4,5,128,128]{3,2,1,0:T(8,128)(2,1)}, u32[]{:S(2)}, u32[]{:S(2)}) collective-permute-start(bf16[4,5,128,128]{3,2,1,0:T(8,128)(2,1)S(1)} %collective-permute-done.17), channel_id=1, source_target_pairs={{0,16},{1,17},{2,18},{3,19},{4,20},{5,21},{6,22},{7,23},{8,24},{9,... | collective-permute-start | bytes 1966088 | tf_op jit(solution)/shard_map/ppermute | solution.py:218
  194.0 0.3 collective-permute-start.26
  194.2 0.4 fusion
  194.6 0.1 broadcast_in_dim.25
  194.7 0.7 reshape_reshape.4.refs_1_
  195.5 0.6 concatenate.15.refs_0_
  196.1 0.6 collective-permute-done.26
  196.8 19.7 %base.1 = f32[2560,1280]{1,0:T(8,128)} custom-call(s32[103]{0:T(128)} %concatenate.15.refs_0_, f32[20,1,1280]{2,1,0:T(1,128)} %reshape_reshape.4.refs_1_, bf16[2560,128]{1,0:T(8,128)(2,1)} %turn.1.refs_2_, bf16[2560,128]{1,0:T(8,128)(2,1)} %collective-permute-done.1.refs_3_, bf16[2560,128]{1,0:T(8,128)(2,1)} %collective-permute-done.2.refs_4_, ...), custom_call_target="tpu_custom_call" | custom-call | flops 6710886400 | bytes 35651584 | tf_op jit(solution)/shard_map/base/pallas_call | solution.py:184
  (66 shorter events, 0.3 us)
Async XLA Ops:
  0.8 1.9 copy-start
  4.9 17.6 %copy-start.4 = (bf16[128,1280]{1,0:T(8,128)(2,1)S(1)}, bf16[128,1280]{1,0:T(8,128)(2,1)}, u32[]{:S(2)}) copy-start(bf16[128,1280]{1,0:T(8,128)(2,1)} %param.14) | copy-start | bytes 983044
  16.4 12.3 %all-to-all-start.3 = ((bf16[4,5,128,128]{3,2,1,0:T(8,128)(2,1)}), bf16[4,5,128,128]{3,2,1,0:T(8,128)(2,1)S(1)}, u32[]{:S(2)}, u32[]{:S(2)}) async-start(bf16[4,5,128,128]{3,2,1,0:T(8,128)(2,1)} %get-tuple-element.13), calls=%async_computation.3 | async-start | bytes 1310720 | tf_op jit(solution)/shard_map/all_to_all | solution.py:262
  22.5 14.6 %collective-permute-start.8 = (bf16[128,1280]{1,0:T(8,128)(2,1)S(1)}, bf16[128,1280]{1,0:T(8,128)(2,1)S(1)}, u32[]{:S(2)}, u32[]{:S(2)}) collective-permute-start(bf16[128,1280]{1,0:T(8,128)(2,1)S(1)} %copy-done.4), channel_id=1, source_target_pairs={{0,32},{1,33},{2,34},{3,35},{4,36},{5,37},{6,38},{7,39},{8,40},{9,... | collective-permute-start | bytes 983048 | tf_op jit(solution)/shard_map/ppermute | solution.py:218
  23.4 14.9 %collective-permute-start = (bf16[64,2560]{1,0:T(8,128)(2,1)}, bf16[64,2560]{1,0:T(8,128)(2,1)}, u32[]{:S(2)}, u32[]{:S(2)}) collective-permute-start(bf16[64,2560]{1,0:T(8,128)(2,1)} %bitcast.5.a), channel_id=1, source_target_pairs={{0,1},{1,0},{2,3},{3,2},{4,5},{5,4},{6,7},{7,6},{8,9},{9,8},{10,11... | collective-permute-start | bytes 983048 | tf_op jit(solution)/shard_map/ppermute | solution.py:218
  28.7 17.5 %all-to-all-start.4 = ((bf16[4,5,128,128]{3,2,1,0:T(8,128)(2,1)}), bf16[4,5,128,128]{3,2,1,0:T(8,128)(2,1)}, u32[]{:S(2)}, u32[]{:S(2)}) async-start(bf16[4,5,128,128]{3,2,1,0:T(8,128)(2,1)} %get-tuple-element.14), calls=%async_computation.4 | async-start | bytes 1310720 | tf_op jit(solution)/shard_map/all_to_all | solution.py:262
  35.5 17.2 %collective-permute-start.11 = (bf16[4,5,128,128]{3,2,1,0:T(8,128)(2,1)S(1)}, bf16[4,5,128,128]{3,2,1,0:T(8,128)(2,1)}, u32[]{:S(2)}, u32[]{:S(2)}) collective-permute-start(bf16[4,5,128,128]{3,2,1,0:T(8,128)(2,1)S(1)} %get-tuple-element.10), channel_id=1, source_target_pairs={{8,0},{0,1},{13,2},{6,3},{5,4},{10,5},{3,6},{15,7},{12,8},{4,9},{9... | collective-permute-start | bytes 1966088 | tf_op jit(solution)/shard_map/ppermute | solution.py:265
  38.0 18.0 %collective-permute-start.9 = (bf16[256,1280]{1,0:T(8,128)(2,1)}, bf16[256,1280]{1,0:T(8,128)(2,1)S(1)}, u32[]{:S(2)}, u32[]{:S(2)}) collective-permute-start(bf16[256,1280]{1,0:T(8,128)(2,1)} %pad_maximum_fusion), channel_id=1, source_target_pairs={{0,96},{1,97},{2,98},{3,99},{4,100},{5,101},{6,102},{7,103},{8,104... | collective-permute-start | bytes 1966088 | tf_op jit(solution)/shard_map/ppermute | solution.py:218
  40.4 25.9 %collective-permute-start.4 = (bf16[2560,128]{1,0:T(8,128)(2,1)}, bf16[2560,128]{1,0:T(8,128)(2,1)}, u32[]{:S(2)}, u32[]{:S(2)}) collective-permute-start(bf16[2560,128]{1,0:T(8,128)(2,1)} %turn.1.refs_2_), channel_id=1, source_target_pairs={{0,12},{1,13},{2,14},{3,15},{4,8},{5,9},{6,10},{7,11},{8,4},{9,5},... | collective-permute-start | bytes 1966088 | tf_op jit(solution)/shard_map/ppermute | solution.py:218
  42.3 31.2 %collective-permute-start.2 = (bf16[2560,128]{1,0:T(8,128)(2,1)}, bf16[2560,128]{1,0:T(8,128)(2,1)}, u32[]{:S(2)}, u32[]{:S(2)}) collective-permute-start(bf16[2560,128]{1,0:T(8,128)(2,1)} %turn.1.refs_2_), channel_id=1, source_target_pairs={{0,4},{1,5},{2,6},{3,7},{4,0},{5,1},{6,2},{7,3},{8,12},{9,13},{10,... | collective-permute-start | bytes 1966088 | tf_op jit(solution)/shard_map/ppermute | solution.py:218
  42.7 38.9 %collective-permute-start.1 = (bf16[2560,128]{1,0:T(8,128)(2,1)}, bf16[2560,128]{1,0:T(8,128)(2,1)}, u32[]{:S(2)}, u32[]{:S(2)}) collective-permute-start(bf16[2560,128]{1,0:T(8,128)(2,1)} %turn.1.refs_2_), channel_id=1, source_target_pairs={{0,3},{1,2},{2,1},{3,0},{4,7},{5,6},{6,5},{7,4},{8,11},{9,10},{10,... | collective-permute-start | bytes 1966088 | tf_op jit(solution)/shard_map/ppermute | solution.py:218
  46.2 27.3 %all-to-all-start.1 = ((bf16[4,5,128,128]{3,2,1,0:T(8,128)(2,1)}), bf16[4,5,128,128]{3,2,1,0:T(8,128)(2,1)}, u32[]{:S(2)}, u32[]{:S(2)}) async-start(bf16[4,5,128,128]{3,2,1,0:T(8,128)(2,1)} %get-tuple-element.11), calls=%async_computation.1 | async-start | bytes 1310720 | tf_op jit(solution)/shard_map/all_to_all | solution.py:262
  52.7 29.0 %collective-permute-start.15 = (bf16[4,5,128,128]{3,2,1,0:T(8,128)(2,1)}, bf16[4,5,128,128]{3,2,1,0:T(8,128)(2,1)}, u32[]{:S(2)}, u32[]{:S(2)}) collective-permute-start(bf16[4,5,128,128]{3,2,1,0:T(8,128)(2,1)} %all-to-all-done.4), channel_id=1, source_target_pairs={{12,0},{6,1},{1,2},{0,3},{3,4},{14,5},{10,6},{11,7},{8,8},{13,9},{... | collective-permute-start | bytes 1966088 | tf_op jit(solution)/shard_map/ppermute | solution.py:265
  56.0 30.2 %collective-permute-start.14 = (bf16[4,5,128,128]{3,2,1,0:T(8,128)(2,1)S(1)}, bf16[4,5,128,128]{3,2,1,0:T(8,128)(2,1)S(1)}, u32[]{:S(2)}, u32[]{:S(2)}) collective-permute-start(bf16[4,5,128,128]{3,2,1,0:T(8,128)(2,1)S(1)} %all-to-all-done.3), channel_id=1, source_target_pairs={{4,0},{1,1},{14,2},{3,3},{11,4},{2,5},{13,6},{8,7},{0,8},{5,9},{10... | collective-permute-start | bytes 1966088 | tf_op jit(solution)/shard_map/ppermute | solution.py:265
  66.3 33.3 %collective-permute-start.13 = (bf16[4,5,128,128]{3,2,1,0:T(8,128)(2,1)S(1)}, bf16[4,5,128,128]{3,2,1,0:T(8,128)(2,1)}, u32[]{:S(2)}, u32[]{:S(2)}) collective-permute-start(bf16[4,5,128,128]{3,2,1,0:T(8,128)(2,1)S(1)} %all_to_all.30), channel_id=1, source_target_pairs={{3,0},{14,1},{9,2},{11,3},{8,4},{6,5},{5,6},{0,7},{7,8},{2,9},{13,... | collective-permute-start | bytes 1966088 | tf_op jit(solution)/shard_map/ppermute | solution.py:265
  73.5 30.7 %collective-permute-start.12 = (bf16[4,5,128,128]{3,2,1,0:T(8,128)(2,1)}, bf16[4,5,128,128]{3,2,1,0:T(8,128)(2,1)S(1)}, u32[]{:S(2)}, u32[]{:S(2)}) collective-permute-start(bf16[4,5,128,128]{3,2,1,0:T(8,128)(2,1)} %all-to-all-done.1), channel_id=1, source_target_pairs={{11,0},{9,1},{5,2},{8,3},{0,4},{13,5},{2,6},{7,7},{15,8},{10,9},{1... | collective-permute-start | bytes 1966088 | tf_op jit(solution)/shard_map/ppermute | solution.py:265
  81.6 31.3 %collective-permute-start.16 = (bf16[4,5,128,128]{3,2,1,0:T(8,128)(2,1)}, bf16[4,5,128,128]{3,2,1,0:T(8,128)(2,1)}, u32[]{:S(2)}, u32[]{:S(2)}) collective-permute-start(bf16[4,5,128,128]{3,2,1,0:T(8,128)(2,1)} %collective-permute-done.11), channel_id=1, source_target_pairs={{0,1},{1,0},{2,3},{3,2},{4,5},{5,4},{6,7},{7,6},{8,9},{9,8},{10,11... | collective-permute-start | bytes 1966088 | tf_op jit(solution)/shard_map/ppermute | solution.py:218
  81.7 54.8 %collective-permute-start.5 = (bf16[2560,128]{1,0:T(8,128)(2,1)}, bf16[2560,128]{1,0:T(8,128)(2,1)}, u32[]{:S(2)}, u32[]{:S(2)}) collective-permute-start(bf16[2560,128]{1,0:T(8,128)(2,1)} %collective-permute-done.1.refs_3_), channel_id=1, source_target_pairs={{0,12},{1,13},{2,14},{3,15},{4,8},{5,9},{6,10},{7,11},{8,4},{9,5},... | collective-permute-start | bytes 1966088 | tf_op jit(solution)/shard_map/ppermute | solution.py:218
  86.2 42.1 %copy-start.5 = (bf16[4,5,128,128]{3,2,1,0:T(8,128)(2,1)}, bf16[4,5,128,128]{3,2,1,0:T(8,128)(2,1)S(1)}, u32[]{:S(2)}) copy-start(bf16[4,5,128,128]{3,2,1,0:T(8,128)(2,1)S(1)} %collective-permute-done.14) | copy-start | bytes 1966084
  86.2 50.4 %collective-permute-start.3 = (bf16[2560,128]{1,0:T(8,128)(2,1)}, bf16[2560,128]{1,0:T(8,128)(2,1)}, u32[]{:S(2)}, u32[]{:S(2)}) collective-permute-start(bf16[2560,128]{1,0:T(8,128)(2,1)} %collective-permute-done.1.refs_3_), channel_id=1, source_target_pairs={{0,4},{1,5},{2,6},{3,7},{4,0},{5,1},{6,2},{7,3},{8,12},{9,13},{10,... | collective-permute-start | bytes 1966088 | tf_op jit(solution)/shard_map/ppermute | solution.py:218
  99.6 36.5 %collective-permute-start.6 = (bf16[2560,128]{1,0:T(8,128)(2,1)}, bf16[2560,128]{1,0:T(8,128)(2,1)}, u32[]{:S(2)}, u32[]{:S(2)}) collective-permute-start(bf16[2560,128]{1,0:T(8,128)(2,1)} %collective-permute-done.2.refs_4_), channel_id=1, source_target_pairs={{0,12},{1,13},{2,14},{3,15},{4,8},{5,9},{6,10},{7,11},{8,4},{9,5},... | collective-permute-start | bytes 1966088 | tf_op jit(solution)/shard_map/ppermute | solution.py:218
  104.2 8.7 %copy-start.7 = (bf16[4,5,128,128]{3,2,1,0:T(8,128)(2,1)}, bf16[4,5,128,128]{3,2,1,0:T(8,128)(2,1)S(1)}, u32[]{:S(2)}) copy-start(bf16[4,5,128,128]{3,2,1,0:T(8,128)(2,1)S(1)} %collective-permute-done.12) | copy-start | bytes 1966084
  104.2 43.4 %collective-permute-start.25 = (bf16[4,5,128,128]{3,2,1,0:T(8,128)(2,1)}, bf16[4,5,128,128]{3,2,1,0:T(8,128)(2,1)}, u32[]{:S(2)}, u32[]{:S(2)}) collective-permute-start(bf16[4,5,128,128]{3,2,1,0:T(8,128)(2,1)} %collective-permute-done.15), channel_id=1, source_target_pairs={{0,16},{1,17},{2,18},{3,19},{4,20},{5,21},{6,22},{7,23},{8,24},{9,... | collective-permute-start | bytes 1966088 | tf_op jit(solution)/shard_map/ppermute | solution.py:218
  112.9 35.5 %collective-permute-start.20 = (bf16[4,5,128,128]{3,2,1,0:T(8,128)(2,1)}, bf16[4,5,128,128]{3,2,1,0:T(8,128)(2,1)}, u32[]{:S(2)}, u32[]{:S(2)}) collective-permute-start(bf16[4,5,128,128]{3,2,1,0:T(8,128)(2,1)} %collective-permute-done.15), channel_id=1, source_target_pairs={{0,1},{1,0},{2,3},{3,2},{4,5},{5,4},{6,7},{7,6},{8,9},{9,8},{10,11... | collective-permute-start | bytes 1966088 | tf_op jit(solution)/shard_map/ppermute | solution.py:218
  128.3 20.1 %copy-start.10 = (s32[8192,2]{0,1:T(2,128)S(1)}, s32[8192,2]{0,1:T(2,128)}, u32[]{:S(2)}) copy-start(s32[8192,2]{0,1:T(2,128)} %param.12) | copy-start | bytes 196612
  128.3 20.1 %copy-start.11 = (s32[2,80]{1,0:T(2,128)S(1)}, s32[2,80]{1,0:T(2,128)}, u32[]{:S(2)}) copy-start(s32[2,80]{1,0:T(2,128)} %param.11) | copy-start | bytes 1924
  128.3 35.3 %all-to-all-start = ((bf16[4,5,128,128]{3,2,1,0:T(8,128)(2,1)}), bf16[4,5,128,128]{3,2,1,0:T(8,128)(2,1)S(1)}, u32[]{:S(2)}, u32[]{:S(2)}) async-start(bf16[4,5,128,128]{3,2,1,0:T(8,128)(2,1)} %collective-permute-done.11), calls=%async_computation | async-start | bytes 1310720 | tf_op jit(solution)/shard_map/all_to_all | solution.py:262
  133.6 3.0 %copy-start.6 = (bf16[4,5,128,128]{3,2,1,0:T(8,128)(2,1)S(1)}, bf16[4,5,128,128]{3,2,1,0:T(8,128)(2,1)}, u32[]{:S(2)}) copy-start(bf16[4,5,128,128]{3,2,1,0:T(8,128)(2,1)} %copy-done.5) | copy-start | bytes 1966084
  133.6 47.7 %copy-start.12 = (s32[2,80]{1,0:T(2,128)S(1)}, s32[2,80]{1,0:T(2,128)}, u32[]{:S(2)}) copy-start(s32[2,80]{1,0:T(2,128)} %param.10) | copy-start | bytes 1924
  133.6 63.1 %copy-start.3 = (bf16[512,1280]{1,0:T(8,128)(2,1)}, bf16[512,1280]{1,0:T(8,128)(2,1)S(1)}, u32[]{:S(2)}) copy-start(bf16[512,1280]{1,0:T(8,128)(2,1)S(1)} %constant_dynamic-update-slice_fusion) | copy-start | bytes 3932164
  133.6 61.8 %copy-start.13 = (s32[16]{0:T(128)S(1)}, s32[16]{0:T(128)}, u32[]{:S(2)}) copy-start(s32[16]{0:T(128)} %constant.34.clone) | copy-start | bytes 196
  136.0 57.9 %collective-permute-start.10 = (bf16[512,1280]{1,0:T(8,128)(2,1)S(1)}, bf16[512,1280]{1,0:T(8,128)(2,1)}, u32[]{:S(2)}, u32[]{:S(2)}) collective-permute-start(bf16[512,1280]{1,0:T(8,128)(2,1)S(1)} %constant_dynamic-update-slice_fusion), channel_id=1, source_target_pairs={{0,16},{1,17},{2,18},{3,19},{4,20},{5,21},{6,22},{7,23},{8,24},{9,... | collective-permute-start | bytes 3932168 | tf_op jit(solution)/shard_map/ppermute | solution.py:218
  136.5 12.2 %collective-permute-start.24 = (bf16[4,5,128,128]{3,2,1,0:T(8,128)(2,1)S(1)}, bf16[4,5,128,128]{3,2,1,0:T(8,128)(2,1)S(1)}, u32[]{:S(2)}, u32[]{:S(2)}) collective-permute-start(bf16[4,5,128,128]{3,2,1,0:T(8,128)(2,1)S(1)} %copy-done.6), channel_id=1, source_target_pairs={{0,16},{1,17},{2,18},{3,19},{4,20},{5,21},{6,22},{7,23},{8,24},{9,... | collective-permute-start | bytes 1966088 | tf_op jit(solution)/shard_map/ppermute | solution.py:218
  136.6 25.8 %collective-permute-start.19 = (bf16[4,5,128,128]{3,2,1,0:T(8,128)(2,1)S(1)}, bf16[4,5,128,128]{3,2,1,0:T(8,128)(2,1)}, u32[]{:S(2)}, u32[]{:S(2)}) collective-permute-start(bf16[4,5,128,128]{3,2,1,0:T(8,128)(2,1)S(1)} %copy-done.6), channel_id=1, source_target_pairs={{0,1},{1,0},{2,3},{3,2},{4,5},{5,4},{6,7},{7,6},{8,9},{9,8},{10,11... | collective-permute-start | bytes 1966088 | tf_op jit(solution)/shard_map/ppermute | solution.py:218
  147.6 16.0 %collective-permute-start.23 = (bf16[4,5,128,128]{3,2,1,0:T(8,128)(2,1)}, bf16[4,5,128,128]{3,2,1,0:T(8,128)(2,1)}, u32[]{:S(2)}, u32[]{:S(2)}) collective-permute-start(bf16[4,5,128,128]{3,2,1,0:T(8,128)(2,1)} %collective-permute-done.13), channel_id=1, source_target_pairs={{0,16},{1,17},{2,18},{3,19},{4,20},{5,21},{6,22},{7,23},{8,24},{9,... | collective-permute-start | bytes 1966088 | tf_op jit(solution)/shard_map/ppermute | solution.py:218
  148.3 28.1 %collective-permute-start.18 = (bf16[4,5,128,128]{3,2,1,0:T(8,128)(2,1)}, bf16[4,5,128,128]{3,2,1,0:T(8,128)(2,1)}, u32[]{:S(2)}, u32[]{:S(2)}) collective-permute-start(bf16[4,5,128,128]{3,2,1,0:T(8,128)(2,1)} %collective-permute-done.13), channel_id=1, source_target_pairs={{0,1},{1,0},{2,3},{3,2},{4,5},{5,4},{6,7},{7,6},{8,9},{9,8},{10,11... | collective-permute-start | bytes 1966088 | tf_op jit(solution)/shard_map/ppermute | solution.py:218
  148.7 27.8 %copy-start.8 = (bf16[4,5,128,128]{3,2,1,0:T(8,128)(2,1)}, bf16[4,5,128,128]{3,2,1,0:T(8,128)(2,1)S(1)}, u32[]{:S(2)}) copy-start(bf16[4,5,128,128]{3,2,1,0:T(8,128)(2,1)S(1)} %collective-permute-done.24) | copy-start | bytes 1966084
  148.7 33.0 %collective-permute-start.22 = (bf16[4,5,128,128]{3,2,1,0:T(8,128)(2,1)}, bf16[4,5,128,128]{3,2,1,0:T(8,128)(2,1)}, u32[]{:S(2)}, u32[]{:S(2)}) collective-permute-start(bf16[4,5,128,128]{3,2,1,0:T(8,128)(2,1)} %copy-done.7), channel_id=1, source_target_pairs={{0,16},{1,17},{2,18},{3,19},{4,20},{5,21},{6,22},{7,23},{8,24},{9,... | collective-permute-start | bytes 1966088 | tf_op jit(solution)/shard_map/ppermute | solution.py:218
  162.4 28.1 %collective-permute-start.17 = (bf16[4,5,128,128]{3,2,1,0:T(8,128)(2,1)}, bf16[4,5,128,128]{3,2,1,0:T(8,128)(2,1)S(1)}, u32[]{:S(2)}, u32[]{:S(2)}) collective-permute-start(bf16[4,5,128,128]{3,2,1,0:T(8,128)(2,1)} %copy-done.7), channel_id=1, source_target_pairs={{0,1},{1,0},{2,3},{3,2},{4,5},{5,4},{6,7},{7,6},{8,9},{9,8},{10,11... | collective-permute-start | bytes 1966088 | tf_op jit(solution)/shard_map/ppermute | solution.py:218
  163.6 33.1 %copy-start.1 = (bf16[4,5,128,128]{3,2,1,0:T(8,128)(2,1)}, bf16[4,5,128,128]{3,2,1,0:T(8,128)(2,1)S(1)}, u32[]{:S(2)}) copy-start(bf16[4,5,128,128]{3,2,1,0:T(8,128)(2,1)S(1)} %all-to-all-done) | copy-start | bytes 1966084
  163.6 27.8 %collective-permute-start.21 = (bf16[4,5,128,128]{3,2,1,0:T(8,128)(2,1)S(1)}, bf16[4,5,128,128]{3,2,1,0:T(8,128)(2,1)}, u32[]{:S(2)}, u32[]{:S(2)}) collective-permute-start(bf16[4,5,128,128]{3,2,1,0:T(8,128)(2,1)S(1)} %all-to-all-done), channel_id=1, source_target_pairs={{0,16},{1,17},{2,18},{3,19},{4,20},{5,21},{6,22},{7,23},{8,24},{9,... | collective-permute-start | bytes 1966088 | tf_op jit(solution)/shard_map/ppermute | solution.py:218
  176.5 15.0 %collective-permute-start.7 = (bf16[2560,128]{1,0:T(8,128)(2,1)}, bf16[2560,128]{1,0:T(8,128)(2,1)}, u32[]{:S(2)}, u32[]{:S(2)}) collective-permute-start(bf16[2560,128]{1,0:T(8,128)(2,1)} %collective-permute-done.5.refs_7_), channel_id=1, source_target_pairs={{0,4},{1,5},{2,6},{3,7},{4,0},{5,1},{6,2},{7,3},{8,12},{9,13},{10,... | collective-permute-start | bytes 1966088 | tf_op jit(solution)/shard_map/ppermute | solution.py:218
  176.5 17.5 %all-to-all-start.5 = ((bf16[4,5,128,128]{3,2,1,0:T(8,128)(2,1)}), bf16[4,5,128,128]{3,2,1,0:T(8,128)(2,1)S(1)}, u32[]{:S(2)}, u32[]{:S(2)}) async-start(bf16[4,5,128,128]{3,2,1,0:T(8,128)(2,1)} %collective-permute-done.16), calls=%async_computation.5 | async-start | bytes 1310720 | tf_op jit(solution)/shard_map/all_to_all | solution.py:262
  181.7 14.4 %collective-permute-start.30 = (bf16[4,5,128,128]{3,2,1,0:T(8,128)(2,1)}, bf16[4,5,128,128]{3,2,1,0:T(8,128)(2,1)}, u32[]{:S(2)}, u32[]{:S(2)}) collective-permute-start(bf16[4,5,128,128]{3,2,1,0:T(8,128)(2,1)} %collective-permute-done.20), channel_id=1, source_target_pairs={{0,16},{1,17},{2,18},{3,19},{4,20},{5,21},{6,22},{7,23},{8,24},{9,... | collective-permute-start | bytes 1966088 | tf_op jit(solution)/shard_map/ppermute | solution.py:218
  190.5 6.2 %copy-start.9 = (bf16[4,5,128,128]{3,2,1,0:T(8,128)(2,1)}, bf16[4,5,128,128]{3,2,1,0:T(8,128)(2,1)S(1)}, u32[]{:S(2)}) copy-start(bf16[4,5,128,128]{3,2,1,0:T(8,128)(2,1)S(1)} %collective-permute-done.17) | copy-start | bytes 1966084
  190.5 5.6 %collective-permute-start.29 = (bf16[4,5,128,128]{3,2,1,0:T(8,128)(2,1)}, bf16[4,5,128,128]{3,2,1,0:T(8,128)(2,1)}, u32[]{:S(2)}, u32[]{:S(2)}) collective-permute-start(bf16[4,5,128,128]{3,2,1,0:T(8,128)(2,1)} %collective-permute-done.19), channel_id=1, source_target_pairs={{0,16},{1,17},{2,18},{3,19},{4,20},{5,21},{6,22},{7,23},{8,24},{9,... | collective-permute-start | bytes 1966088 | tf_op jit(solution)/shard_map/ppermute | solution.py:218
  191.4 4.7 %collective-permute-start.28 = (bf16[4,5,128,128]{3,2,1,0:T(8,128)(2,1)}, bf16[4,5,128,128]{3,2,1,0:T(8,128)(2,1)}, u32[]{:S(2)}, u32[]{:S(2)}) collective-permute-start(bf16[4,5,128,128]{3,2,1,0:T(8,128)(2,1)} %collective-permute-done.18), channel_id=1, source_target_pairs={{0,16},{1,17},{2,18},{3,19},{4,20},{5,21},{6,22},{7,23},{8,24},{9,... | collective-permute-start | bytes 1966088 | tf_op jit(solution)/shard_map/ppermute | solution.py:218
  191.5 4.6 %collective-permute-start.27 = (bf16[4,5,128,128]{3,2,1,0:T(8,128)(2,1)S(1)}, bf16[4,5,128,128]{3,2,1,0:T(8,128)(2,1)}, u32[]{:S(2)}, u32[]{:S(2)}) collective-permute-start(bf16[4,5,128,128]{3,2,1,0:T(8,128)(2,1)S(1)} %collective-permute-done.17), channel_id=1, source_target_pairs={{0,16},{1,17},{2,18},{3,19},{4,20},{5,21},{6,22},{7,23},{8,24},{9,... | collective-permute-start | bytes 1966088 | tf_op jit(solution)/shard_map/ppermute | solution.py:218
  193.9 2.8 %copy-start.2 = (bf16[4,5,128,128]{3,2,1,0:T(8,128)(2,1)}, bf16[4,5,128,128]{3,2,1,0:T(8,128)(2,1)S(1)}, u32[]{:S(2)}) copy-start(bf16[4,5,128,128]{3,2,1,0:T(8,128)(2,1)S(1)} %all-to-all-done.5) | copy-start | bytes 1966084
  194.0 2.8 %collective-permute-start.26 = (bf16[4,5,128,128]{3,2,1,0:T(8,128)(2,1)S(1)}, bf16[4,5,128,128]{3,2,1,0:T(8,128)(2,1)}, u32[]{:S(2)}, u32[]{:S(2)}) collective-permute-start(bf16[4,5,128,128]{3,2,1,0:T(8,128)(2,1)S(1)} %all-to-all-done.5), channel_id=1, source_target_pairs={{0,16},{1,17},{2,18},{3,19},{4,20},{5,21},{6,22},{7,23},{8,24},{9,... | collective-permute-start | bytes 1966088 | tf_op jit(solution)/shard_map/ppermute | solution.py:218
